TPU v7x, 512 devices: a whole 4x8x8 slice. The times are simulated.
512 devices in a mesh: seq: 64 (over z, x, core), exp: 8 (over y).
Axes of the slice: x: 4, y: 8, z: 8, core: 2. Of those that a mesh axis runs over, the one named last changes fastest.
Arguments:
- inner_x: bfloat16 [8192, 8192], P('seq', 'exp'), may hold values from -6 to 6
- inner_z: bfloat16 [8192, 8192], P('seq', 'exp'), may hold values from -6 to 6
- step_raw: bfloat16 [8192, 8192], P('seq', 'exp'), may hold values from -4.5 to 3
- conv_weight: float32 [4, 8192], P(None, 'exp'), may hold values from -3 to 3
- state_proj: bfloat16 [8192, 32], P('exp'), may hold values from -0.125 to 0.125
- step_bias: float32 [8192], P('exp'), may hold values from -7 to -2.3
- decay_log: float32 [16, 8192], P(None, 'exp'), may hold values from -4 to 2.8
- skip_gain: float32 [8192], P('exp'), may hold values from 0.5 to 1.5
- moe_tokens: bfloat16 [8192, 4096], P('seq', 'exp'), may hold values from -6 to 6
- routes: int32 [8192, 2], P('seq'), may hold values from 0 to 15, all different within a row; in each aligned block of 128 rows (0 to 127, 128 to 255, ...) at most 20 rows name the same one
- gate_weight: bfloat16 [8, 12288, 4096], P('exp', 'seq'), may hold values from -0.09375 to 0.09375
- up_weight: bfloat16 [8, 12288, 4096], P('exp', 'seq'), may hold values from -0.09375 to 0.09375
Outputs:
- mixed: bfloat16 [8192, 8192], P('seq', 'exp')
- hidden: bfloat16 [8, 12288, 1280], P('exp', 'seq')
Inputs may be any that keep to these rules, and one draw needn't show every extreme that they name: `routes`: in each aligned block of 128 rows (the tokens of one device), no expert is named by more than 20 rows, a bound that some block reaches; the two choices of a token differ.
All inputs are finite; a program needn't handle non-finite values.
Results may differ from a plain program's by a relative error of at most 0.0051.
Values may be sent and summed in bfloat16 or wider, within the bound.
No kernel may reach another device: no remote copies, remote signals or barrier semaphores. Data moves between devices by JAX's collectives and lax.ppermute only.
A program may use at most 128 MiB of HBM per device.

v0:
```python
import jax
import jax.numpy as jnp
from jax import lax
from jax.sharding import PartitionSpec as P

CAP = 20


def from_behind(value, axis, steps):
    count = lax.axis_size(axis)
    first, last = (max(0, -steps), min(count, count - steps))
    return lax.ppermute(value, axis, [(source, source + steps) for source in range(first, last)])


def carried_in(value, axis, join, neutral):
    count, mine = (lax.axis_size(axis), lax.axis_index(axis))
    pieces = jax.tree.map(lambda part: lax.all_gather(part, axis), value)
    so_far = jax.tree.map(
        lambda part, zero: jnp.full_like(part, 0) + jnp.asarray(zero, part.dtype), value, neutral
    )

    def turn(position, so_far):
        longer = join(so_far, jax.tree.map(lambda part: part[position], pieces))
        return jax.tree.map(lambda new, old: jnp.where(position < mine, new, old), longer, so_far)

    return lax.fori_loop(0, count - 1, turn, so_far)


def pair_combine(earlier, later):
    return (earlier[0] * later[0], later[0] * earlier[1] + later[1])


def expand_rows(slot_rows, gate_matrix, up_matrix):
    dims = (((1,), (1,)), ((), ()))
    gate_part = lax.dot_general(gate_matrix, slot_rows, dims, preferred_element_type=jnp.float32)
    up_part = lax.dot_general(up_matrix, slot_rows, dims, preferred_element_type=jnp.float32)
    return (jax.nn.silu(gate_part) * up_part).astype(jnp.bfloat16)


def slot_table(pair_ids, experts_count, capacity, tokens):
    onehot = (pair_ids[:, None] == jnp.arange(experts_count, dtype=jnp.int32)[None, :]).astype(
        jnp.int32
    )
    before = jnp.cumsum(onehot, axis=0) - onehot
    places = (before[:, :, None] == jnp.arange(capacity, dtype=jnp.int32)[None, None, :]).astype(
        jnp.int32
    )
    chosen = onehot[:, :, None] * places
    return jnp.sum(chosen.reshape(tokens, -1, experts_count * capacity), axis=1)


def shards(
    inner_x,
    inner_z,
    step_raw,
    conv_weight,
    state_proj,
    step_bias,
    decay_log,
    skip_gain,
    moe_tokens,
    routes,
    gate_weight,
    up_weight,
):
    length = inner_x.shape[0]
    taps = conv_weight.shape[0]
    states = decay_log.shape[0]
    rim_rows = from_behind(inner_x[length - (taps - 1) :], "seq", 1)
    padded = jnp.concatenate([rim_rows, inner_x], axis=0).astype(jnp.float32)
    conv_sum = jnp.zeros(inner_x.shape, jnp.float32)
    for offset in range(taps):
        conv_sum = conv_sum + conv_weight[offset][None, :] * padded[offset : offset + length]
    conv_out = jax.nn.silu(conv_sum)
    partial_coef = jnp.dot(
        conv_out.astype(jnp.bfloat16), state_proj, preferred_element_type=jnp.float32
    )
    coeffs = lax.psum(partial_coef, "exp")
    input_coef = coeffs[:, :states]
    output_coef = coeffs[:, states:]
    step_size = jax.nn.softplus(step_raw.astype(jnp.float32) + step_bias[None, :])
    rates = -jnp.exp(decay_log)
    cumulative = jnp.cumsum(step_size, axis=0)
    total_step = cumulative[-1]
    end_decay = jnp.exp(rates * total_step[None, :])
    remaining = total_step[None, :] - cumulative
    weighted_input = step_size * conv_out
    end_state = jnp.sum(
        jnp.exp(rates[None, :, :] * remaining[:, None, :])
        * input_coef[:, :, None]
        * weighted_input[:, None, :],
        axis=0,
    )
    flight = lax.axis_size("exp")
    table = slot_table(routes.reshape(-1), flight, CAP, routes.shape[0])
    placed = jnp.dot(
        table.T.astype(jnp.bfloat16), moe_tokens, preferred_element_type=jnp.float32
    ).astype(jnp.bfloat16)
    placed = placed.reshape(flight, CAP, moe_tokens.shape[1])
    identity = (jnp.ones(end_decay.shape, jnp.float32), jnp.zeros(end_state.shape, jnp.float32))
    _, incoming = carried_in((end_decay, end_state), "seq", pair_combine, identity)

    def advance(state, row):
        step_row, in_row, out_row, drive_row = row
        state = jnp.exp(rates * step_row[None, :]) * state + in_row[:, None] * drive_row[None, :]
        return (state, jnp.sum(out_row[:, None] * state, axis=0))

    _, scan_out = lax.scan(
        advance, incoming, (step_size, input_coef, output_coef, weighted_input), unroll=8
    )
    result = (scan_out + skip_gain[None, :] * conv_out) * jax.nn.silu(inner_z.astype(jnp.float32))
    mixed = result.astype(jnp.bfloat16)
    arrived = lax.all_to_all(placed, "exp", split_axis=0, concat_axis=2, tiled=True)
    hidden = expand_rows(
        lax.all_gather(arrived[0], "seq", axis=0, tiled=True), gate_weight[0], up_weight[0]
    )[None]
    return (mixed, hidden)


def solution(mesh):
    return jax.shard_map(
        shards,
        mesh=mesh,
        in_specs=(
            P("seq", "exp"),
            P("seq", "exp"),
            P("seq", "exp"),
            P(None, "exp"),
            P("exp", None),
            P("exp"),
            P(None, "exp"),
            P("exp"),
            P("seq", "exp"),
            P("seq", None),
            P("exp", "seq", None),
            P("exp", "seq", None),
        ),
        out_specs=(P("seq", "exp"), P("exp", "seq", None)),
        check_vma=False,
    )
```

profile of v0, /device:TPU:1, one launch (start us, length us, event | category | flops | bytes accessed | tf_op | source)
XLA Modules:
  0.0 357.7 jit_solution(17284810150058443251)
XLA Ops:
  8.1 4.5 %collective-permute-start = (bf16[3,1024]{1,0:T(4,128)(2,1)S(1)}, bf16[3,1024]{1,0:T(4,128)(2,1)S(1)}, u32[]{:S(2)}, u32[]{:S(2)}) collective-permute-start(bf16[3,1024]{1,0:T(4,128)(2,1)S(1)} %slice.172), channel_id=1, source_target_pairs={{0,8},{8,16},{16,24},{24,32},{32,40},{40,48},{48,56},{56,64},{64,7... | collective-permute-start | bytes 18440 | tf_op jit(solution)/shard_map/ppermute | solution.py:12
  13.5 3.4 collective-permute-done
  16.9 1.0 maximum_convert_fusion
  17.9 2.6 fusion.21
  21.0 1.5 exponential_negate_fusion
  22.5 1.0 fusion.15
  23.6 20.1 %psum.7 = f32[128,32]{0,1:T(8,128)S(1)} all-reduce(f32[128,32]{0,1:T(8,128)S(1)} %fusion.15), channel_id=1, replica_groups=mesh['seq'=64,'exp'=8] {'exp'}, use_global_device_ids=true, to_apply=%region_1.2 | all-reduce | flops 4096 | bytes 32768 | tf_op jit(solution)/shard_map/psum | solution.py:78
  43.8 3.5 multiply_reduce_fusion.8
  51.2 1.2 mul.472
  52.4 1.2 mul.473
  53.7 1.4 fusion.14
  55.1 1.1 convolution_convert_fusion
  56.9 3.8 %all-to-all-start = ((bf16[8,20,512]{2,1,0:T(8,128)(2,1)}), bf16[8,20,512]{2,1,0:T(8,128)(2,1)S(1)}, u32[]{:S(2)}, u32[]{:S(2)}) async-start(bf16[8,20,512]{2,1,0:T(8,128)(2,1)} %reshape.175), calls=%async_computation | async-start | bytes 393216 | tf_op jit(solution)/shard_map/all_to_all | solution.py:113
  61.1 8.3 %all-to-all-done = bf16[8,20,512]{2,1,0:T(8,128)(2,1)S(1)} async-done(((bf16[8,20,512]{2,1,0:T(8,128)(2,1)}), bf16[8,20,512]{2,1,0:T(8,128)(2,1)S(1)}, u32[]{:S(2)}, u32[]{:S(2)}) %all-to-all-start) | async-done | bytes 163872 | tf_op jit(solution)/shard_map/all_to_all | solution.py:113
  70.2 72.7 %all-gather.9.cloned.1.call-done = f32[1024,1024]{1,0:T(8,128)} async-done(((f32[16,1024]{1,0:T(8,128)}), f32[1024,1024]{1,0:T(8,128)}) %all-gather.9.cloned.1.call-update) | async-done | bytes 4194320 | tf_op jit(solution)/shard_map/all_gather | solution.py:17
  142.9 85.3 %all-gather.7.cloned.1.call-done = f32[1024,1024]{1,0:T(8,128)} async-done(((f32[16,1024]{1,0:T(8,128)}), f32[1024,1024]{1,0:T(8,128)}) %all-gather.7.cloned.1.call-update) | async-done | bytes 4194320 | tf_op jit(solution)/shard_map/all_gather | solution.py:17
  228.3 59.1 %while.27 = (s32[]{:T(128)}, f32[16,1024]{1,0:T(8,128)S(1)}, s32[]{:T(128)}, f32[64,16,1024]{2,1,0:T(8,128)}, f32[64,16,1024]{2,1,0:T(8,128)}, /*index=5*/s32[]{:T(128)}, s32[]{:T(128)}) while((s32[]{:T(128)}, f32[16,1024]{1,0:T(8,128)S(1)}, s32[]{:T(128)}, f32[64,16,1024]{2,1,0:T(8,128)}, f32[64,16,1024]{2,1,0:T(8,128)}, ...), condition=%wide.region_4.5_spmd.clone, body=%wide.region_3.4_spmd.clone.sunk | while | flops 65540 | bytes 262245 | solution.py:26
  229.2 0.9 fusion.29
  230.1 0.9 fusion.29
  231.1 0.9 fusion.29
  232.0 0.9 fusion.29
  232.9 0.9 fusion.29
  233.9 0.9 fusion.29
  234.8 0.9 fusion.29
  235.8 0.9 fusion.29
  236.7 0.9 fusion.29
  237.6 0.9 fusion.29
  242.3 0.9 fusion.29
  243.2 0.9 fusion.29
  244.2 0.9 fusion.29
  247.0 0.9 fusion.29
  249.8 0.9 fusion.29
  252.6 0.9 fusion.29
  253.6 0.9 fusion.29
  256.4 0.9 fusion.29
  259.2 0.9 fusion.29
  261.1 0.9 fusion.29
  263.0 0.9 fusion.29
  265.8 0.9 fusion.29
  272.3 0.9 fusion.29
  273.3 0.9 fusion.29
  281.7 0.9 fusion.29
  284.5 1.0 fusion.29
  287.4 30.8 %while.26 = (s32[]{:T(128)}, f32[16,1024]{1,0:T(8,128)S(1)}, f32[16,8,1024]{2,1,0:T(8,128)S(1)}, f32[16,8,1024]{2,1,0:T(8,128)}, f32[16,1024]{1,0:T(8,128)S(1)},...) while((s32[]{:T(128)}, f32[16,1024]{1,0:T(8,128)S(1)}, ...), condition=%wide.region_14.15_spmd, body=%wide.region_5.14_spmd.sunk | while | flops 1171465 | bytes 939673 | solution.py:108
  287.4 1.3 constant_dynamic-slice_fusion.21
  289.3 1.4 constant_dynamic-slice_fusion.21
  291.3 1.3 constant_dynamic-slice_fusion.21
  293.2 1.3 constant_dynamic-slice_fusion.21
  295.1 1.3 constant_dynamic-slice_fusion.21
  297.0 1.3 constant_dynamic-slice_fusion.21
  298.9 1.3 constant_dynamic-slice_fusion.21
  300.8 1.3 constant_dynamic-slice_fusion.21
  302.7 1.5 constant_dynamic-slice_fusion.21
  304.9 1.3 constant_dynamic-slice_fusion.21
  306.8 1.3 constant_dynamic-slice_fusion.21
  308.7 1.3 constant_dynamic-slice_fusion.21
  310.6 1.3 constant_dynamic-slice_fusion.21
  312.5 1.3 constant_dynamic-slice_fusion.21
  314.4 1.3 constant_dynamic-slice_fusion.21
  316.3 1.3 constant_dynamic-slice_fusion.21
  319.1 5.9 %all-gather.11.cloned.1.call-done = bf16[64,20,4096]{2,1,0:T(8,128)(2,1)} async-done(((bf16[1,20,4096]{2,1,0:T(8,128)(2,1)}), bf16[64,20,4096]{2,1,0:T(8,128)(2,1)}) %all-gather.11.cloned.1.call-update) | async-done | bytes 10485776 | tf_op jit(solution)/shard_map/all_gather | solution.py:115
  325.0 14.0 %reshape.179 = bf16[1280,4096]{1,0:T(8,128)(2,1)} reshape(bf16[64,20,4096]{2,1,0:T(8,128)(2,1)} %all-gather.11.cloned.1.call-done) | data formatting | bytes 20971520
  339.0 7.7 %convolution_bitcast_fusion.1 = f32[192,1280]{1,0:T(8,128)S(1)} fusion(bf16[1280,4096]{1,0:T(8,128)(2,1)} %reshape.179, bf16[1,192,4096]{2,1,0:T(8,128)(2,1)S(1)} %copy-done), kind=kOutput, calls=%fused_computation.57 | convolution fusion | flops 2013265920 | bytes 13041664 | tf_op jit(solution)/shard_map/dot_general | solution.py:35
  346.8 4.4 %fusion.3 = bf16[1,192,1280]{2,1,0:T(8,128)(2,1)} fusion(bf16[1280,4096]{1,0:T(8,128)(2,1)S(1)} %copy-done.1, bf16[1,192,4096]{2,1,0:T(8,128)(2,1)S(1)} %copy-done.5, f32[192,1280]{1,0:T(8,128)S(1)} %convolution_bitcast_fusion.1), kind=kOutput, calls=%fused_computation.59 | convolution fusion | flops 2014740480 | bytes 13533184 | tf_op jit(solution)/shard_map/dot_general | solution.py:36
  (213 shorter events, 51.7 us)
Async XLA Ops:
  7.2 331.9 %copy-start = (bf16[1,192,4096]{2,1,0:T(8,128)(2,1)S(1)}, bf16[1,192,4096]{2,1,0:T(8,128)(2,1)}, u32[]{:S(2)}) copy-start(bf16[1,192,4096]{2,1,0:T(8,128)(2,1)} %param.26) | copy-start | bytes 4718596
  7.2 40.9 %copy-start.4 = (s32[128,2]{0,1:T(2,128)S(1)}, s32[128,2]{0,1:T(2,128)}, u32[]{:S(2)}) copy-start(s32[128,2]{0,1:T(2,128)} %param.25) | copy-start | bytes 3076
  7.2 135.7 %all-gather.9.cloned.1.call-start = ((), (), s32[]{:S(2)}) async-start(), calls=%async_computation.2 | async-start | bytes 4259840 | tf_op jit(solution)/shard_map/all_gather | solution.py:17
  8.1 8.8 %collective-permute-start = (bf16[3,1024]{1,0:T(4,128)(2,1)S(1)}, bf16[3,1024]{1,0:T(4,128)(2,1)S(1)}, u32[]{:S(2)}, u32[]{:S(2)}) collective-permute-start(bf16[3,1024]{1,0:T(4,128)(2,1)S(1)} %slice.172), channel_id=1, source_target_pairs={{0,8},{8,16},{16,24},{24,32},{32,40},{40,48},{48,56},{56,64},{64,7... | collective-permute-start | bytes 18440 | tf_op jit(solution)/shard_map/ppermute | solution.py:12
  47.3 271.0 %copy-start.3 = (f32[1024]{0:T(1024)S(1)}, f32[1024]{0:T(1024)}, u32[]{:S(2)}) copy-start(f32[1024]{0:T(1024)} %param.23) | copy-start | bytes 12292
  47.3 181.0 %all-gather.7.cloned.1.call-start = ((), (), s32[]{:S(2)}) async-start(), calls=%async_computation.1 | async-start | bytes 4259840 | tf_op jit(solution)/shard_map/all_gather | solution.py:17
  53.6 264.6 %copy-start.2 = (bf16[128,1024]{1,0:T(8,128)(2,1)S(1)}, bf16[128,1024]{1,0:T(8,128)(2,1)}, u32[]{:S(2)}) copy-start(bf16[128,1024]{1,0:T(8,128)(2,1)} %param.17) | copy-start | bytes 786436
  56.9 12.4 %all-to-all-start = ((bf16[8,20,512]{2,1,0:T(8,128)(2,1)}), bf16[8,20,512]{2,1,0:T(8,128)(2,1)S(1)}, u32[]{:S(2)}, u32[]{:S(2)}) async-start(bf16[8,20,512]{2,1,0:T(8,128)(2,1)} %reshape.175), calls=%async_computation | async-start | bytes 393216 | tf_op jit(solution)/shard_map/all_to_all | solution.py:113
  60.7 264.3 %all-gather.11.cloned.1.call-start = ((), (), s32[]{:S(2)}) async-start(), calls=%async_computation.3 | async-start | bytes 12779520 | tf_op jit(solution)/shard_map/all_gather | solution.py:115
  339.0 7.7 %copy-start.1 = (bf16[1280,4096]{1,0:T(8,128)(2,1)S(1)}, bf16[1280,4096]{1,0:T(8,128)(2,1)}, u32[]{:S(2)}) copy-start(bf16[1280,4096]{1,0:T(8,128)(2,1)} %reshape.179) | copy-start | bytes 31457284
  339.0 7.7 %copy-start.5 = (bf16[1,192,4096]{2,1,0:T(8,128)(2,1)S(1)}, bf16[1,192,4096]{2,1,0:T(8,128)(2,1)}, u32[]{:S(2)}) copy-start(bf16[1,192,4096]{2,1,0:T(8,128)(2,1)} %param.27) | copy-start | bytes 4718596
Sparse Core Ops, SparseCore 0:
  47.4 95.4 all-gather.8
  146.3 81.9 all-gather.6
  232.2 92.7 all-gather.10
where the time goes:
time: 363 us; the launch traced here: 358 us
  waiting for transfers between devices  176 us (48%)
  other arithmetic  77 us (21%)
  local copies, waits for them, and re-layouts  45.2 us (12%)
  blocking collectives  20.1 us (6%)
  matrix products  14.2 us (4%)
  between operations  13.9 us (4%)
  starting transfers between devices  8.55 us (2%)
    all_gather x2, waiting for transfers between devices, carried_in(): pieces = jax.tree.map(lambda part: lax.all_gather(part, axis), value)  158 us
    select_n x63, other arithmetic, turn(): jnp.where(position < mine, new, old)  57.8 us
    slice x16, local copies, waits for them, and re-layouts, shards(): lax.scan(advance, incoming, (step_size, input_coef, output_coef, weighted...  21.1 us
    psum x1, blocking collectives, shards(): coeffs = lax.psum(partial_coef, 'exp')  20.1 us
    unnamed x15, local copies, waits for them, and re-layouts  14.9 us
    all_to_all x1, waiting for transfers between devices, shards(): lax.all_to_all(placed, 'exp', split_axis=0, concat_axis=2, tiled=True)  8.28 us
    dot_general x1, matrix products, expand_rows(): lax.dot_general(gate_matrix, slot_rows, dims, preferred_element_type=jnp....  7.72 us
  transfers between devices with their start and end apart: 5, of which 5 were waited for; matrix products, arithmetic and copies ran while one was open for 28% of the time, Pallas kernels for 0%

commit v1 on v0

v1 whole, which is shorter than its diff:
```python
import functools

import jax
import jax.numpy as jnp
from jax import lax
from jax.experimental import pallas as pl
from jax.experimental.pallas import tpu as pltpu
from jax.sharding import Mesh
from jax.sharding import PartitionSpec as P

CAP = 20
F32 = jnp.float32
BF16 = jnp.bfloat16
LOG2E = 1.4426950408889634
SEQ = ("z", "x", "c")

VMEM = pl.BlockSpec(memory_space=pltpu.VMEM)
SMEM = pl.BlockSpec(memory_space=pltpu.SMEM)


def call(kernel, out_shape, in_specs, scratch=(), name=None):
    return pl.pallas_call(
        kernel,
        out_shape=out_shape,
        in_specs=in_specs,
        out_specs=jax.tree.map(lambda _: VMEM, out_shape),
        scratch_shapes=scratch,
        name=name,
        compiler_params=pltpu.CompilerParams(vmem_limit_bytes=48 << 20),
    )


def shape(dims, dtype):
    return jax.ShapeDtypeStruct(dims, dtype)


def place_kernel(routes_ref, tokens_ref, out_ref):
    rows = tokens_ref.shape[0]
    column = lax.broadcasted_iota(jnp.int32, (rows, 256), 1)
    expert, slot = column >> 5, column & 31
    named = (routes_ref[:, 0:1] == expert) | (routes_ref[:, 1:2] == expert)
    earlier = lax.broadcasted_iota(jnp.int32, (rows, rows), 0) > lax.broadcasted_iota(
        jnp.int32, (rows, rows), 1
    )
    before = jnp.dot(
        jnp.where(earlier, 1.0, 0.0).astype(BF16),
        jnp.where(named, 1.0, 0.0).astype(BF16),
        preferred_element_type=F32,
    )
    table = jnp.where(named & (before == slot.astype(F32)), 1.0, 0.0).astype(BF16)
    placed = lax.dot_general(
        table, tokens_ref[...], (((0,), (0,)), ((), ())), preferred_element_type=F32
    ).astype(BF16)
    for index in range(8):
        out_ref[index] = placed[index * 32 : index * 32 + CAP]


def silu(value):
    return value / (1.0 + jnp.exp(-value))


def softplus(value):
    small = jnp.exp(-jnp.abs(value))
    ratio = small / (2.0 + small)
    square = ratio * ratio
    series = jnp.full_like(square, 1.0 / 15.0)
    for odd in (13, 11, 9, 7, 5, 3):
        series = series * square + 1.0 / odd
    return jnp.maximum(value, 0.0) + 2.0 * ratio * (series * square + 1.0)


def conv_kernel(
    x_ref,
    rim_ref,
    raw_ref,
    weight_ref,
    proj_ref,
    bias_ref,
    decay_ref,
    conv_ref,
    step_ref,
    drive_ref,
    rate_ref,
    part_ref,
    padded,
):
    rows, width = x_ref.shape
    padded[8:, :] = x_ref[...].astype(F32)
    padded[5:8, :] = rim_ref[...].astype(F32)
    total = jnp.zeros((rows, width), F32)
    for tap in range(4):
        total = total + weight_ref[tap : tap + 1, :] * padded[5 + tap : 5 + tap + rows, :]
    conv = silu(total)
    conv_ref[...] = conv
    part = lax.dot_general(
        proj_ref[...], conv.astype(BF16), (((0,), (1,)), ((), ())), preferred_element_type=F32
    )
    for index in range(8):
        part_ref[index] = part
    step = softplus(raw_ref[...].astype(F32) + bias_ref[...])
    drive = step * conv
    rate = -jnp.exp(decay_ref[...]) * LOG2E
    for index in range(width // 128):
        lanes = slice(index * 128, index * 128 + 128)
        step_ref[pl.ds(index, rows, stride=8), :] = step[:, lanes]
        drive_ref[pl.ds(index, rows, stride=8), :] = drive[:, lanes]
        rate_ref[pl.ds(index, rate.shape[0], stride=8), :] = rate[:, lanes]


def pack_state(states, total):
    high = total.astype(BF16).astype(F32)
    middle = (total - high).astype(BF16).astype(F32)
    low = total - high - middle
    tail = jnp.concatenate([high, middle, low, jnp.zeros_like(total)], axis=0)
    return jnp.concatenate(list(states) + [tail], axis=0).astype(BF16)


def unpack_state(ref, position):
    block = ref[position].astype(F32)
    states = [block[n * 8 : n * 8 + 8] for n in range(16)]
    return states, block[128:136] + block[136:144] + block[144:152]


def scan_kernel(coef_ref, step_ref, drive_ref, rate_ref, y_ref, sum_ref, end_ref):
    rows = step_ref.shape[0] // 8
    rates = [rate_ref[n * 8 : n * 8 + 8, :] for n in range(16)]
    zero = jnp.zeros((8, 128), F32)

    def advance(token, carry):
        total, states = carry
        here = pl.ds(pl.multiple_of(token * 8, 8), 8)
        step, drive = step_ref[here, :], drive_ref[here, :]
        total = total + step
        sum_ref[here, :] = total
        parts, following = [zero, zero], []
        for n in range(16):
            state = jnp.exp2(rates[n] * step) * states[n] + coef_ref[n, token] * drive
            parts[n % 2] = parts[n % 2] + coef_ref[16 + n, token] * state
            following.append(state)
        y_ref[here, :] = parts[0] + parts[1]
        return total, tuple(following)

    total, states = lax.fori_loop(0, rows, advance, (zero, (zero,) * 16), unroll=4)
    packed = pack_state(states, total)
    for index in range(8):
        end_ref[index] = packed


def fold(ref, rates, limit, states, total):
    for position in range(8):
        more, step = unpack_state(ref, position)
        keep = position < limit
        states = [
            jnp.where(keep, jnp.exp2(rates[n] * step) * states[n] + more[n], states[n])
            for n in range(16)
        ]
        total = jnp.where(keep, total + step, total)
    return states, total


def group_kernel(mine_ref, got_ref, rate_ref, before_ref, step_ref, all_ref):
    rates = [rate_ref[n * 8 : n * 8 + 8, :] for n in range(16)]
    zero = jnp.zeros((8, 128), F32)
    states, total = fold(got_ref, rates, mine_ref[0], [zero] * 16, zero)
    for n in range(16):
        before_ref[n * 8 : n * 8 + 8, :] = states[n]
    step_ref[...] = total
    states, total = fold(got_ref, rates, 8, [zero] * 16, zero)
    packed = pack_state(states, total)
    for index in range(8):
        all_ref[index] = packed


def finish_kernel(
    mine_ref,
    coef_ref,
    got_ref,
    rate_ref,
    before_ref,
    before_step_ref,
    y_ref,
    sum_ref,
    conv_ref,
    gain_ref,
    z_ref,
    out_ref,
    dense,
):
    rows, width = conv_ref.shape
    rates = [rate_ref[n * 8 : n * 8 + 8, :] for n in range(16)]
    zero = jnp.zeros((8, 128), F32)
    states, _ = fold(got_ref, rates, mine_ref[0], [zero] * 16, zero)
    states = [
        jnp.exp2(rates[n] * before_step_ref[...]) * states[n] + before_ref[n * 8 : n * 8 + 8, :]
        for n in range(16)
    ]

    def advance(token, carry):
        here = pl.ds(pl.multiple_of(token * 8, 8), 8)
        total = sum_ref[here, :]
        parts = [y_ref[here, :], zero]
        for n in range(16):
            parts[n % 2] = parts[n % 2] + coef_ref[16 + n, token] * (
                jnp.exp2(rates[n] * total) * states[n]
            )
        dense[here, :] = parts[0] + parts[1]
        return carry

    lax.fori_loop(0, rows, advance, 0, unroll=4)
    for index in range(width // 128):
        lanes = slice(index * 128, index * 128 + 128)
        value = dense[pl.ds(index, rows, stride=8), :]
        value = value + gain_ref[:, lanes] * conv_ref[:, lanes]
        out_ref[:, lanes] = (value * silu(z_ref[:, lanes].astype(F32))).astype(BF16)


def expand_rows(slot_rows, gate_matrix, up_matrix):
    dims = (((1,), (1,)), ((), ()))
    gate_part = lax.dot_general(gate_matrix, slot_rows, dims, preferred_element_type=F32)
    up_part = lax.dot_general(up_matrix, slot_rows, dims, preferred_element_type=F32)
    return (jax.nn.silu(gate_part) * up_part).astype(BF16)


def shards(
    inner_x,
    inner_z,
    step_raw,
    conv_weight,
    state_proj,
    step_bias,
    decay_log,
    skip_gain,
    moe_tokens,
    routes,
    gate_weight,
    up_weight,
):
    rows, width = inner_x.shape
    shards_of = lax.axis_size(SEQ)
    rim = lax.ppermute(inner_x[rows - 3 :], SEQ, [(i, i + 1) for i in range(shards_of - 1)])
    placed = call(place_kernel, shape((8, CAP, moe_tokens.shape[1]), BF16), [VMEM] * 2, name="place")(
        routes, moe_tokens
    )
    arrived = lax.all_to_all(placed, "exp", split_axis=0, concat_axis=2, tiled=True)
    gathered = lax.all_gather(arrived[0], SEQ, axis=0, tiled=True)

    dense = shape((rows * width // 128, 128), F32)
    conv, step, drive, rate, part = call(
        conv_kernel,
        (
            shape((rows, width), F32),
            dense,
            dense,
            shape((128, 128), F32),
            shape((8, 32, rows), F32),
        ),
        [VMEM] * 7,
        [pltpu.VMEM((rows + 8, width), F32)],
        name="conv",
    )(inner_x, rim, step_raw, conv_weight, state_proj, step_bias[None], decay_log)
    coef = jnp.sum(lax.all_to_all(part, "exp", split_axis=0, concat_axis=0, tiled=True), axis=0)
    packed = shape((8, 160, 128), BF16)
    local, sums, ends = call(
        scan_kernel, (dense, dense, packed), [SMEM] + [VMEM] * 3, name="scan"
    )(coef, step, drive, rate)
    near = lax.all_to_all(ends, ("x", "c"), split_axis=0, concat_axis=0, tiled=True)
    place_in = lax.axis_index(("x", "c")).astype(jnp.int32).reshape(1)
    before, before_step, whole = call(
        group_kernel,
        (shape((128, 128), F32), shape((8, 128), F32), packed),
        [SMEM, VMEM, VMEM],
        name="group",
    )(place_in, near, rate)
    far = lax.all_to_all(whole, "z", split_axis=0, concat_axis=0, tiled=True)
    layer = lax.axis_index("z").astype(jnp.int32).reshape(1)
    mixed = call(
        finish_kernel,
        shape((rows, width), BF16),
        [SMEM, SMEM] + [VMEM] * 9,
        [pltpu.VMEM(dense.shape, F32)],
        name="finish",
    )(layer, coef, far, rate, before, before_step, local, sums, conv, skip_gain[None], inner_z)

    hidden = expand_rows(gathered, gate_weight[0], up_weight[0])[None]
    return mixed, hidden


def solution(mesh):
    fine = Mesh(mesh.devices.reshape(8, 4, 2, 8), ("z", "x", "c", "exp"))
    return jax.shard_map(
        shards,
        mesh=fine,
        in_specs=(
            P(SEQ, "exp"),
            P(SEQ, "exp"),
            P(SEQ, "exp"),
            P(None, "exp"),
            P("exp", None),
            P("exp"),
            P(None, "exp"),
            P("exp"),
            P(SEQ, "exp"),
            P(SEQ, None),
            P("exp", SEQ, None),
            P("exp", SEQ, None),
        ),
        out_specs=(P(SEQ, "exp"), P("exp", SEQ, None)),
        check_vma=False,
    )
```

time: 363 us -> 160 us (0.44); the launches traced: 358 us -> 159 us
  waiting for transfers between devices: 176 us -> 42.3 us
  other arithmetic: 77 us -> 0.01 us
  local copies, waits for them, and re-layouts: 45.2 us -> 27.8 us
  starting transfers between devices: 8.55 us -> 24.2 us
  Pallas kernels: 0 us -> 11.6 us
  blocking collectives: 20.1 us -> 26.8 us
    all_gather x3 -> x1, waiting for transfers between devices: 164 us -> 18.8 us  [shards(): gathered = lax.all_gather(arrived[0], SEQ, axis=0, tiled=True)]
    select_n x63 -> x0, other arithmetic: 57.8 us -> none  [turn(): jnp.where(position < mine, new, old)]
    all_to_all x0 -> x2, blocking collectives: none -> 26.8 us  [the longest x1 16.2 us: shards(): lax.all_to_all(placed, 'exp', split_axis=0, concat_axis=2, tiled=True)]
    slice x23 -> x1, local copies, waits for them, and re-layouts: 23.3 us -> 0.73 us  [shards(): inner_x[rows - 3:]]
    psum x1 -> x0, blocking collectives: 20.1 us -> none  [shards(): coeffs = lax.psum(partial_coef, 'exp')]
    all_to_all x1 -> x2, waiting for transfers between devices: 8.28 us -> 23.5 us  [the longest x1 16.4 us: shards(): far = lax.all_to_all(whole, 'z', split_axis=0, concat_axis=0, tiled=True)]
    all_to_all x1 -> x2, starting transfers between devices: 3.76 us -> 18.4 us  [the longest x1 11.9 us: shards(): far = lax.all_to_all(whole, 'z', split_axis=0, concat_axis=0, tiled=True)]
    unnamed x15 -> x34, local copies, waits for them, and re-layouts: 14.9 us -> 27.1 us
  transfers between devices with their start and end apart: 5 -> 4, of which waited for: 5 -> 3; matrix products, arithmetic and copies ran while one was open for 28% -> 1% of each run, Pallas kernels for 0% -> 7%
where the time goes in v1:
time: 160 us; the launch traced here: 159 us
  waiting for transfers between devices  42.3 us (26%)
  local copies, waits for them, and re-layouts  27.8 us (17%)
  blocking collectives  26.8 us (17%)
  starting transfers between devices  24.2 us (15%)
  between operations  14.1 us (9%)
  matrix products  12.1 us (8%)
  Pallas kernels  11.6 us (7%)
    unnamed x34, local copies, waits for them, and re-layouts  27.1 us
    all_gather x1, waiting for transfers between devices, shards(): gathered = lax.all_gather(arrived[0], SEQ, axis=0, tiled=True)  18.8 us
    all_to_all x1, waiting for transfers between devices, shards(): far = lax.all_to_all(whole, 'z', split_axis=0, concat_axis=0, tiled=True)  16.4 us
    all_to_all x1, blocking collectives, shards(): lax.all_to_all(placed, 'exp', split_axis=0, concat_axis=2, tiled=True)  16.2 us
    all_to_all x1, starting transfers between devices, shards(): far = lax.all_to_all(whole, 'z', split_axis=0, concat_axis=0, tiled=True)  11.9 us
    all_to_all x1, blocking collectives, shards(): lax.all_to_all(part, 'exp', split_axis=0, concat_axis=0, tiled=True)  10.6 us
    dot_general x1, matrix products, expand_rows(): lax.dot_general(gate_matrix, slot_rows, dims, preferred_element_type=F32)  7.72 us
    all_to_all x1, waiting for transfers between devices, shards(): lax.all_to_all(ends, ('x', 'c'), split_axis=0, concat_axis=0, tiled=True)  7.12 us
  transfers between devices with their start and end apart: 4, of which 3 were waited for; matrix products, arithmetic and copies ran while one was open for 1% of the time, Pallas kernels for 7%

profile of v1, /device:TPU:1, one launch (start us, length us, event | category | flops | bytes accessed | tf_op | source)
XLA Modules:
  0.0 159.0 jit_solution(16146876587975669984)
XLA Ops:
  7.2 0.0 copy-start
  7.2 0.0 all-gather.3.cloned.1.call-start
  7.2 0.9 copy.20.routes_ref
  8.1 0.0 copy-start.8
  8.1 0.9 copy-done.8
  9.0 0.5 place.1
  9.5 16.2 %all_to_all.30 = bf16[8,20,512]{2,1,0:T(8,128)(2,1)S(1)} all-to-all(bf16[8,20,512]{2,1,0:T(8,128)(2,1)S(1)} %place.1), channel_id=1, replica_groups=mesh['z'=8,'x'=4,'c'=2,'exp'=8] {'exp'}, dimensions={0} | all-to-all | bytes 327680 | tf_op jit(solution)/shard_map/all_to_all | solution.py:244
  25.7 0.1 copy.21
  25.8 0.8 reshape.13
  26.5 0.0 all-gather.3.cloned.1.call-update
  26.6 0.7 slice.3
  27.3 5.7 %collective-permute-start = (bf16[3,1024]{1,0:T(4,128)(2,1)S(1)}, bf16[3,1024]{1,0:T(4,128)(2,1)S(1)}, u32[]{:S(2)}, u32[]{:S(2)}) collective-permute-start(bf16[3,1024]{1,0:T(4,128)(2,1)S(1)} %slice.3), channel_id=1, source_target_pairs={{0,8},{8,16},{16,24},{24,32},{32,40},{40,48},{48,56},{56,64},{64,7... | collective-permute-start | bytes 18440 | tf_op jit(solution)/shard_map/ppermute | solution.py:240
  33.0 1.0 copy.19.proj_ref
  34.0 0.0 collective-permute-done.rim_ref
  34.0 0.0 copy-start.5
  34.0 0.9 copy-done.5
  35.0 0.0 copy-start.6
  35.0 0.9 copy-done.6
  35.9 0.0 copy-start.9
  35.9 0.8 copy-done.9
  36.8 0.0 copy-start.10
  36.8 0.7 copy-done.10
  37.5 0.0 copy-start.11
  37.5 0.7 copy-done.11
  38.2 1.2 conv.1
  39.4 10.6 %all_to_all.31 = f32[8,32,128]{2,1,0:T(8,128)S(1)} all-to-all(f32[8,32,128]{2,1,0:T(8,128)S(1)} %get-tuple-element.13), channel_id=1, replica_groups=mesh['z'=8,'x'=4,'c'=2,'exp'=8] {'exp'}, dimensions={0} | all-to-all | bytes 262144 | tf_op jit(solution)/shard_map/all_to_all | solution.py:261
  50.0 5.2 %scan.1 = (f32[1024,128]{1,0:T(8,128)S(1)}, f32[1024,128]{1,0:T(8,128)S(1)}, bf16[8,160,128]{2,1,0:T(8,128)(2,1)}) custom-call(f32[32,128]{1,0:T(8,128)S(1)} %reduce_sum.9.coef_ref, f32[1024,128]{1,0:T(8,128)S(1)} %get-tuple-element.14.step_ref, f32[1024,128]{1,0:T(8,128)S(1)} %get-tuple-element.15.drive_ref, f32[128,128]{1,0:T(8,128)S(1)} %get-tuple-element.16.rate_ref), custom_call_target="tpu_custom_call" | custom-call | tf_op jit(solution)/shard_map/scan/pallas_call | solution.py:263
  55.2 0.0 copy-start.1
  55.2 0.8 copy-done.1
  56.1 0.0 copy-start.3
  56.1 0.8 copy-done.3
  56.9 6.6 %all-to-all-start.1 = ((bf16[8,160,128]{2,1,0:T(8,128)(2,1)}), bf16[8,160,128]{2,1,0:T(8,128)(2,1)S(1)}, u32[]{:S(2)}, u32[]{:S(2)}) async-start(bf16[8,160,128]{2,1,0:T(8,128)(2,1)} %get-tuple-element.17), calls=%async_computation.1 | async-start | bytes 655360 | tf_op jit(solution)/shard_map/all_to_all | solution.py:266
  63.5 7.1 %all-to-all-done.1.got_ref = bf16[8,160,128]{2,1,0:T(8,128)(2,1)S(1)} async-done(((bf16[8,160,128]{2,1,0:T(8,128)(2,1)}), bf16[8,160,128]{2,1,0:T(8,128)(2,1)S(1)}, u32[]{:S(2)}, u32[]{:S(2)}) %all-to-all-start.1) | async-done | bytes 327712 | tf_op jit(solution)/shard_map/all_to_all | solution.py:266
  70.6 0.8 group.1
  71.4 11.9 %all-to-all-start.2 = ((bf16[8,160,128]{2,1,0:T(8,128)(2,1)}), bf16[8,160,128]{2,1,0:T(8,128)(2,1)S(1)}, u32[]{:S(2)}, u32[]{:S(2)}) async-start(bf16[8,160,128]{2,1,0:T(8,128)(2,1)} %get-tuple-element.18), calls=%async_computation.2 | async-start | bytes 655360 | tf_op jit(solution)/shard_map/all_to_all | solution.py:274
  83.3 16.4 %all-to-all-done.2.got_ref = bf16[8,160,128]{2,1,0:T(8,128)(2,1)S(1)} async-done(((bf16[8,160,128]{2,1,0:T(8,128)(2,1)}), bf16[8,160,128]{2,1,0:T(8,128)(2,1)S(1)}, u32[]{:S(2)}, u32[]{:S(2)}) %all-to-all-start.2) | async-done | bytes 327712 | tf_op jit(solution)/shard_map/all_to_all | solution.py:274
  99.6 0.0 copy-start.2
  99.6 1.1 copy-done.2
  100.7 0.0 copy-start.4
  100.7 1.0 copy-done.4
  101.7 0.0 copy-start.7
  101.7 0.9 copy-done.7
  102.7 0.0 copy-start.12
  102.7 0.7 copy-done.12
  103.4 3.9 %finish.1 = bf16[128,1024]{1,0:T(8,128)(2,1)} custom-call(s32[1]{0:T(128)} %bitcast.mine_ref, f32[32,128]{1,0:T(8,128)S(1)} %reduce_sum.9.coef_ref, bf16[8,160,128]{2,1,0:T(8,128)(2,1)S(1)} %all-to-all-done.2.got_ref, f32[128,128]{1,0:T(8,128)S(1)} %get-tuple-element.16.rate_ref, f32[128,128]{1,0:T(8,128)S(1)} %get-tuple-element.19.before_ref, ...), custom_call_target="tpu_custom_call" | custom-call | tf_op jit(solution)/shard_map/finish/pallas_call | solution.py:276
  107.2 18.8 %all-gather.3.cloned.1.call-done = bf16[64,20,4096]{2,1,0:T(8,128)(2,1)} async-done(((bf16[1,20,4096]{2,1,0:T(8,128)(2,1)}), bf16[64,20,4096]{2,1,0:T(8,128)(2,1)}) %all-gather.3.cloned.1.call-update) | async-done | bytes 10485776 | tf_op jit(solution)/shard_map/all_gather | solution.py:245
  126.0 13.9 %reshape.14 = bf16[1280,4096]{1,0:T(8,128)(2,1)} reshape(bf16[64,20,4096]{2,1,0:T(8,128)(2,1)} %all-gather.3.cloned.1.call-done) | data formatting | bytes 20971520
  140.0 0.0 copy-done
  140.0 0.0 copy-start.13
  140.0 0.0 copy-start.14
  140.0 7.7 %convolution_bitcast_fusion.1 = f32[192,1280]{1,0:T(8,128)S(1)} fusion(bf16[1280,4096]{1,0:T(8,128)(2,1)} %reshape.14, bf16[1,192,4096]{2,1,0:T(8,128)(2,1)S(1)} %copy-done), kind=kOutput, calls=%fused_computation.2 | convolution fusion | flops 2013265920 | bytes 13041664 | tf_op jit(solution)/shard_map/dot_general | solution.py:219
  147.7 0.0 copy-done.13
  147.7 0.0 copy-done.14
  147.7 4.4 %fusion.2 = bf16[1,192,1280]{2,1,0:T(8,128)(2,1)} fusion(bf16[1280,4096]{1,0:T(8,128)(2,1)S(1)} %copy-done.13, bf16[1,192,4096]{2,1,0:T(8,128)(2,1)S(1)} %copy-done.14, f32[192,1280]{1,0:T(8,128)S(1)} %convolution_bitcast_fusion.1), kind=kOutput, calls=%fused_computation.4 | convolution fusion | flops 2014740480 | bytes 13533184 | tf_op jit(solution)/shard_map/dot_general | solution.py:220
  (1 shorter events, 0.0 us)
Async XLA Ops:
  7.2 132.8 %copy-start = (bf16[1,192,4096]{2,1,0:T(8,128)(2,1)S(1)}, bf16[1,192,4096]{2,1,0:T(8,128)(2,1)}, u32[]{:S(2)}) copy-start(bf16[1,192,4096]{2,1,0:T(8,128)(2,1)} %param.22) | copy-start | bytes 4718596
  7.2 118.9 %all-gather.3.cloned.1.call-start = ((), (), s32[]{:S(2)}) async-start(), calls=%async_computation.4 | async-start | bytes 12779520 | tf_op jit(solution)/shard_map/all_gather | solution.py:245
  8.1 0.9 copy-start.8
  27.3 6.7 %collective-permute-start = (bf16[3,1024]{1,0:T(4,128)(2,1)S(1)}, bf16[3,1024]{1,0:T(4,128)(2,1)S(1)}, u32[]{:S(2)}, u32[]{:S(2)}) collective-permute-start(bf16[3,1024]{1,0:T(4,128)(2,1)S(1)} %slice.3), channel_id=1, source_target_pairs={{0,8},{8,16},{16,24},{24,32},{32,40},{40,48},{48,56},{56,64},{64,7... | collective-permute-start | bytes 18440 | tf_op jit(solution)/shard_map/ppermute | solution.py:240
  34.0 1.0 copy-start.5
  35.0 0.9 copy-start.6
  35.9 0.8 copy-start.9
  36.8 0.7 copy-start.10
  37.5 0.7 copy-start.11
  55.2 0.9 copy-start.1
  56.1 0.8 copy-start.3
  56.9 13.7 %all-to-all-start.1 = ((bf16[8,160,128]{2,1,0:T(8,128)(2,1)}), bf16[8,160,128]{2,1,0:T(8,128)(2,1)S(1)}, u32[]{:S(2)}, u32[]{:S(2)}) async-start(bf16[8,160,128]{2,1,0:T(8,128)(2,1)} %get-tuple-element.17), calls=%async_computation.1 | async-start | bytes 655360 | tf_op jit(solution)/shard_map/all_to_all | solution.py:266
  71.4 28.2 %all-to-all-start.2 = ((bf16[8,160,128]{2,1,0:T(8,128)(2,1)}), bf16[8,160,128]{2,1,0:T(8,128)(2,1)S(1)}, u32[]{:S(2)}, u32[]{:S(2)}) async-start(bf16[8,160,128]{2,1,0:T(8,128)(2,1)} %get-tuple-element.18), calls=%async_computation.2 | async-start | bytes 655360 | tf_op jit(solution)/shard_map/all_to_all | solution.py:274
  99.6 1.1 copy-start.2
  100.7 1.0 copy-start.4
  101.7 0.9 copy-start.7
  102.7 0.7 copy-start.12
  140.0 7.7 %copy-start.13 = (bf16[1280,4096]{1,0:T(8,128)(2,1)S(1)}, bf16[1280,4096]{1,0:T(8,128)(2,1)}, u32[]{:S(2)}) copy-start(bf16[1280,4096]{1,0:T(8,128)(2,1)} %reshape.14) | copy-start | bytes 31457284
  140.0 7.7 %copy-start.14 = (bf16[1,192,4096]{2,1,0:T(8,128)(2,1)S(1)}, bf16[1,192,4096]{2,1,0:T(8,128)(2,1)}, u32[]{:S(2)}) copy-start(bf16[1,192,4096]{2,1,0:T(8,128)(2,1)} %param.23) | copy-start | bytes 4718596
Sparse Core Ops, SparseCore 0:
  26.7 99.2 all-gather.2

commit v2 on v1

--- a/solution.py
+++ b/solution.py
@@ -14,11 +14,14 @@
 LOG2E = 1.4426950408889634
 SEQ = ("z", "x", "c")
 
+FIRST = 12
+REST = CAP - FIRST
+
 VMEM = pl.BlockSpec(memory_space=pltpu.VMEM)
 SMEM = pl.BlockSpec(memory_space=pltpu.SMEM)
 
 
-def call(kernel, out_shape, in_specs, scratch=(), name=None):
+def call(kernel, out_shape, in_specs, scratch=(), name=None, vmem=16, flops=0):
     return pl.pallas_call(
         kernel,
         out_shape=out_shape,
@@ -26,7 +29,8 @@
         out_specs=jax.tree.map(lambda _: VMEM, out_shape),
         scratch_shapes=scratch,
         name=name,
-        compiler_params=pltpu.CompilerParams(vmem_limit_bytes=48 << 20),
+        compiler_params=pltpu.CompilerParams(vmem_limit_bytes=vmem << 20),
+        cost_estimate=pl.CostEstimate(flops=flops, transcendentals=0, bytes_accessed=4 << 20),
     )
 
 
@@ -34,10 +38,11 @@
     return jax.ShapeDtypeStruct(dims, dtype)
 
 
-def place_kernel(routes_ref, tokens_ref, out_ref):
+def place_kernel(routes_ref, tokens_ref, first_ref, rest_ref):
     rows = tokens_ref.shape[0]
     column = lax.broadcasted_iota(jnp.int32, (rows, 256), 1)
     expert, slot = column >> 5, column & 31
+    slot = jnp.where(slot < 16, slot, slot - 16 + FIRST)
     named = (routes_ref[:, 0:1] == expert) | (routes_ref[:, 1:2] == expert)
     earlier = lax.broadcasted_iota(jnp.int32, (rows, rows), 0) > lax.broadcasted_iota(
         jnp.int32, (rows, rows), 1
@@ -52,7 +57,80 @@
         table, tokens_ref[...], (((0,), (0,)), ((), ())), preferred_element_type=F32
     ).astype(BF16)
     for index in range(8):
-        out_ref[index] = placed[index * 32 : index * 32 + CAP]
+        start = index * 32
+        for copy in range(4):
+            first_ref[index * 4 + copy] = placed[start : start + FIRST]
+        for copy in range(8):
+            rest_ref[index * 8 + copy] = placed[start + 16 : start + 16 + REST]
+
+
+def assemble_kernel(got_ref, out_ref, wide):
+    slots = got_ref.shape[1]
+    peers = got_ref.shape[0] // 8
+    for block in range(8):
+        for peer in range(peers):
+            wide[peer * slots : peer * slots + slots, block * 512 : block * 512 + 512] = got_ref[
+                block * peers + peer
+            ].astype(F32)
+    out_ref[...] = wide[...].astype(BF16)
+
+
+def assemble(got, name):
+    dims = (got.shape[0] // 8 * got.shape[1], 4096)
+    return call(
+        assemble_kernel, shape(dims, BF16), [VMEM], [pltpu.VMEM(dims, F32)], name=name, flops=1 << 28
+    )(got)
+
+
+def expand_kernel(gate_ref, up_ref, other_gate_ref, other_up_ref, *refs):
+    dims = (((1,), (1,)), ((), ()))
+    rows_refs, out_refs = refs[:-2], refs[-2:]
+    pairs = ((gate_ref, up_ref), (other_gate_ref, other_up_ref))
+    for (gate, up), out_ref in zip(pairs, out_refs):
+        start = 0
+        for rows_ref in rows_refs:
+            count = rows_ref.shape[0]
+            rows = rows_ref[...]
+            gated = lax.dot_general(gate[...], rows, dims, preferred_element_type=F32)
+            upped = lax.dot_general(up[...], rows, dims, preferred_element_type=F32)
+            out_ref[:, start : start + count] = (silu(gated) * upped).astype(BF16)
+            start += count
+
+
+def expand(weights, blocks, name):
+    units, rows = weights[0].shape[0], sum(block.shape[0] for block in blocks)
+    return call(
+        expand_kernel,
+        (shape((units, rows), BF16),) * 2,
+        [VMEM] * (4 + len(blocks)),
+        name=name,
+        vmem=32,
+        flops=8 * units * rows * 4096,
+    )(*weights, *blocks)
+
+
+def order_kernel(x_ref, core_ref, first_ref, rest_ref, other_first_ref, other_rest_ref, out_ref):
+    columns = out_ref.shape[1]
+    total = jnp.zeros(out_ref.shape, F32)
+    sets = ((first_ref, rest_ref, core_ref[0]), (other_first_ref, other_rest_ref, 1 - core_ref[0]))
+    for early_ref, late_ref, core in sets:
+        for ref in (early_ref, late_ref):
+            count = ref.shape[1]
+            row = lax.broadcasted_iota(jnp.int32, (count, 1), 0)
+            if ref is early_ref:
+                layer, rest = row // (4 * FIRST), row % (4 * FIRST)
+                across, slot = rest // FIRST, rest % FIRST
+            else:
+                block, rest = row // (8 * REST), row % (8 * REST)
+                layer, slot = rest // REST, rest % REST + FIRST
+                shift = jnp.where(block == 0, 0, jnp.where(block == 1, 3, jnp.where(block == 2, 1, 2)))
+                across = (x_ref[0] + shift) & 3
+            column = ((layer * 4 + across) * 2 + core) * CAP + slot
+            table = lax.broadcasted_iota(jnp.int32, (count, columns), 1) == column
+            total = total + jnp.dot(
+                ref[...], jnp.where(table, 1.0, 0.0).astype(BF16), preferred_element_type=F32
+            )
+    out_ref[...] = total.astype(BF16)
 
 
 def silu(value):
@@ -214,13 +292,6 @@
         out_ref[:, lanes] = (value * silu(z_ref[:, lanes].astype(F32))).astype(BF16)
 
 
-def expand_rows(slot_rows, gate_matrix, up_matrix):
-    dims = (((1,), (1,)), ((), ()))
-    gate_part = lax.dot_general(gate_matrix, slot_rows, dims, preferred_element_type=F32)
-    up_part = lax.dot_general(up_matrix, slot_rows, dims, preferred_element_type=F32)
-    return (jax.nn.silu(gate_part) * up_part).astype(BF16)
-
-
 def shards(
     inner_x,
     inner_z,
@@ -238,11 +309,26 @@
     rows, width = inner_x.shape
     shards_of = lax.axis_size(SEQ)
     rim = lax.ppermute(inner_x[rows - 3 :], SEQ, [(i, i + 1) for i in range(shards_of - 1)])
-    placed = call(place_kernel, shape((8, CAP, moe_tokens.shape[1]), BF16), [VMEM] * 2, name="place")(
-        routes, moe_tokens
-    )
-    arrived = lax.all_to_all(placed, "exp", split_axis=0, concat_axis=2, tiled=True)
-    gathered = lax.all_gather(arrived[0], SEQ, axis=0, tiled=True)
+    swap, ahead, back = [(0, 1), (1, 0)], *([(i, (i + d) % 4) for i in range(4)] for d in (1, 3))
+    features = moe_tokens.shape[1]
+    first, rest = call(
+        place_kernel,
+        (shape((32, FIRST, features), BF16), shape((64, REST, features), BF16)),
+        [VMEM] * 2,
+        name="place",
+        flops=1 << 28,
+    )(routes, moe_tokens)
+    first = lax.all_to_all(first, ("exp", "x"), split_axis=0, concat_axis=0, tiled=True)
+    rest = lax.all_to_all(rest, ("exp", "z"), split_axis=0, concat_axis=0, tiled=True)
+    first = lax.all_gather(assemble(first, "assemble_first"), "z", axis=0, tiled=True)
+    rest = assemble(rest, "assemble_rest")
+    half = rest.shape[0] // 2
+    left = lax.ppermute(rest, "x", ahead)
+    right = lax.ppermute(rest, "x", back)
+    far_left = lax.ppermute(left[:half], "x", ahead)
+    far_right = lax.ppermute(right[half:], "x", back)
+    weights = [gate_weight[0], up_weight[0]]
+    weights = weights + [lax.ppermute(weight, "c", swap) for weight in weights]
 
     dense = shape((rows * width // 128, 128), F32)
     conv, step, drive, rate, part = call(
@@ -256,12 +342,12 @@
         ),
         [VMEM] * 7,
         [pltpu.VMEM((rows + 8, width), F32)],
-        name="conv",
+        name="conv", flops=1 << 29,
     )(inner_x, rim, step_raw, conv_weight, state_proj, step_bias[None], decay_log)
     coef = jnp.sum(lax.all_to_all(part, "exp", split_axis=0, concat_axis=0, tiled=True), axis=0)
     packed = shape((8, 160, 128), BF16)
     local, sums, ends = call(
-        scan_kernel, (dense, dense, packed), [SMEM] + [VMEM] * 3, name="scan"
+        scan_kernel, (dense, dense, packed), [SMEM] + [VMEM] * 3, name="scan", flops=1 << 31
     )(coef, step, drive, rate)
     near = lax.all_to_all(ends, ("x", "c"), split_axis=0, concat_axis=0, tiled=True)
     place_in = lax.axis_index(("x", "c")).astype(jnp.int32).reshape(1)
@@ -269,7 +355,7 @@
         group_kernel,
         (shape((128, 128), F32), shape((8, 128), F32), packed),
         [SMEM, VMEM, VMEM],
-        name="group",
+        name="group", flops=1 << 28,
     )(place_in, near, rate)
     far = lax.all_to_all(whole, "z", split_axis=0, concat_axis=0, tiled=True)
     layer = lax.axis_index("z").astype(jnp.int32).reshape(1)
@@ -278,10 +364,22 @@
         shape((rows, width), BF16),
         [SMEM, SMEM] + [VMEM] * 9,
         [pltpu.VMEM(dense.shape, F32)],
-        name="finish",
+        name="finish", flops=1 << 31,
     )(layer, coef, far, rate, before, before_step, local, sums, conv, skip_gain[None], inner_z)
 
-    hidden = expand_rows(gathered, gate_weight[0], up_weight[0])[None]
+    mine_rest, theirs_rest = expand(weights, [rest, left, right, far_left, far_right], "expand_rest")
+    mine, theirs = expand(weights, [first], "expand_first")
+    other_rest = lax.ppermute(theirs_rest, "c", swap)
+    other = lax.ppermute(theirs, "c", swap)
+    here = [lax.axis_index(axis).astype(jnp.int32).reshape(1) for axis in ("x", "c")]
+    units = gate_weight.shape[1]
+    hidden = call(
+        order_kernel,
+        shape((units, 1280), BF16),
+        [SMEM, SMEM] + [VMEM] * 4,
+        name="order",
+        flops=1 << 28,
+    )(*here, mine, mine_rest, other, other_rest)[None]
     return mixed, hidden
 
 

time: 160 us -> 169 us (1.056)
  waiting for transfers between devices: 42.3 us -> 0.07 us
  starting transfers between devices: 24.2 us -> 62.3 us
  Pallas kernels: 11.6 us -> 34.8 us
  matrix products: 12.1 us -> 0 us
    ppermute x0 -> x8, starting transfers between devices: none -> 25.3 us  [the longest x2 6.74 us: shards(): weights = weights + [lax.ppermute(weight, 'c', swap) for weight in weights]]
    pallas_call x2 -> x7, Pallas kernels: 5.67 us -> 28.8 us  [the longest x2 18.1 us: expand(): call(expand_kernel, (shape((units, rows), BF16),) * 2, [VMEM] * (4 + len(...]
    all_to_all x0 -> x2, starting transfers between devices: none -> 19 us  [the longest x1 12.5 us: shards(): lax.all_to_all(rest, ('exp', 'z'), split_axis=0, concat_axis=0, tiled=True)]
    all_gather x1, waiting for transfers between devices: 18.8 us -> 0.02 us  [shards(): lax.all_gather(assemble(first, 'assemble_first'), 'z', axis=0, tiled=True)]
    all_to_all x1, waiting for transfers between devices: 16.4 us -> 0.01 us  [shards(): far = lax.all_to_all(whole, 'z', split_axis=0, concat_axis=0, tiled=True)]
    dot_general x2 -> x0, matrix products: 12.1 us -> none  [the longest x1 7.72 us: expand_rows(): lax.dot_general(gate_matrix, slot_rows, dims, preferred_element_type=F32)]
    all_to_all x1, waiting for transfers between devices: 7.12 us -> 0.01 us  [shards(): lax.all_to_all(ends, ('x', 'c'), split_axis=0, concat_axis=0, tiled=True)]
    slice x0 -> x2, local copies, waits for them, and re-layouts: none -> 3.33 us  [the longest x1 1.67 us: shards(): far_left = lax.ppermute(left[:half], 'x', ahead)]
  transfers between devices with their start and end apart: 4 -> 14, of which waited for: 3 -> 0; matrix products, arithmetic and copies ran while one was open for 1% -> 3% of each run, Pallas kernels for 7% -> 18%
where the time goes in v2:
time: 169 us; the launch traced here: 167 us
  starting transfers between devices  62.3 us (37%)
  Pallas kernels  34.8 us (21%)
  local copies, waits for them, and re-layouts  28.7 us (17%)
  blocking collectives  26.8 us (16%)
  between operations  14.4 us (9%)
    all_to_all x1, blocking collectives, shards(): lax.all_to_all(first, ('exp', 'x'), split_axis=0, concat_axis=0, tiled=True)  26.8 us
    unnamed x74, local copies, waits for them, and re-layouts  24.7 us
    pallas_call x2, Pallas kernels, expand(): call(expand_kernel, (shape((units, rows), BF16),) * 2, [VMEM] * (4 + len(...  18.1 us
    all_to_all x1, starting transfers between devices, shards(): lax.all_to_all(rest, ('exp', 'z'), split_axis=0, concat_axis=0, tiled=True)  12.5 us
    all_to_all x1, starting transfers between devices, shards(): far = lax.all_to_all(whole, 'z', split_axis=0, concat_axis=0, tiled=True)  9.74 us
    ppermute x2, starting transfers between devices, shards(): weights = weights + [lax.ppermute(weight, 'c', swap) for weight in weights]  6.74 us
    all_to_all x1, starting transfers between devices, shards(): lax.all_to_all(part, 'exp', split_axis=0, concat_axis=0, tiled=True)  6.5 us
    all_to_all x1, starting transfers between devices, shards(): lax.all_to_all(ends, ('x', 'c'), split_axis=0, concat_axis=0, tiled=True)  5.72 us
  transfers between devices with their start and end apart: 14, of which 0 were waited for; matrix products, arithmetic and copies ran while one was open for 3% of the time, Pallas kernels for 18%

profile of v2, /device:TPU:1, one launch (start us, length us, event | category | flops | bytes accessed | tf_op | source)
XLA Modules:
  0.0 167.1 jit_solution(4539121620555577597)
XLA Ops:
  7.2 0.0 all-gather.2.cloned.1.call-start
  7.2 0.8 copy.15.routes_ref
  8.0 0.9 copy-done.11
  8.9 0.5 place.1
  9.4 0.8 copy-done.3
  10.3 26.8 %all_to_all.25.got_ref = bf16[32,12,512]{2,1,0:T(8,128)(2,1)S(1)} all-to-all(bf16[32,12,512]{2,1,0:T(8,128)(2,1)S(1)} %get-tuple-element.30), channel_id=1, replica_groups=mesh['z'=8,'x'=4,'c'=2,'exp'=8] {'exp','x'}, dimensions={0} | all-to-all | bytes 786432 | tf_op jit(solution)/shard_map/all_to_all | solution.py:321
  37.1 0.8 assemble_first.1
  37.9 0.0 all-gather.2.cloned.1.call-update
  37.9 12.5 %all-to-all-start.4 = ((bf16[64,8,512]{2,1,0:T(8,128)(2,1)}), bf16[64,8,512]{2,1,0:T(8,128)(2,1)}, u32[]{:S(2)}, u32[]{:S(2)}) async-start(bf16[64,8,512]{2,1,0:T(8,128)(2,1)} %copy-done.3), calls=%async_computation.4 | async-start | bytes 1048576 | tf_op jit(solution)/shard_map/all_to_all | solution.py:322
  50.5 4.8 %collective-permute-start.1 = (bf16[192,4096]{1,0:T(8,128)(2,1)S(1)}, bf16[192,4096]{1,0:T(8,128)(2,1)}, u32[]{:S(2)}, u32[]{:S(2)}) collective-permute-start(bf16[192,4096]{1,0:T(8,128)(2,1)S(1)} %bitcast.9), channel_id=1, source_target_pairs={{0,8},{8,0},{1,9},{9,1},{2,10},{10,2},{3,11},{11,3},{4,12},{12,4},... | collective-permute-start | bytes 4718600 | tf_op jit(solution)/shard_map/ppermute | solution.py:331
  55.3 1.9 %collective-permute-start.2 = (bf16[192,4096]{1,0:T(8,128)(2,1)S(1)}, bf16[192,4096]{1,0:T(8,128)(2,1)}, u32[]{:S(2)}, u32[]{:S(2)}) collective-permute-start(bf16[192,4096]{1,0:T(8,128)(2,1)S(1)} %bitcast.12), channel_id=1, source_target_pairs={{0,8},{8,0},{1,9},{9,1},{2,10},{10,2},{3,11},{11,3},{4,12},{12,4},... | collective-permute-start | bytes 4718600 | tf_op jit(solution)/shard_map/ppermute | solution.py:331
  57.2 0.7 slice.9
  58.0 2.5 %collective-permute-start = (bf16[3,1024]{1,0:T(4,128)(2,1)S(1)}, bf16[3,1024]{1,0:T(4,128)(2,1)S(1)}, u32[]{:S(2)}, u32[]{:S(2)}) collective-permute-start(bf16[3,1024]{1,0:T(4,128)(2,1)S(1)} %slice.9), channel_id=1, source_target_pairs={{0,8},{8,16},{16,24},{24,32},{32,40},{40,48},{48,56},{56,64},{64,7... | collective-permute-start | bytes 18440 | tf_op jit(solution)/shard_map/ppermute | solution.py:311
  60.5 1.0 copy.14.proj_ref
  61.5 0.0 collective-permute-done.rim_ref
  61.5 0.0 copy-start.6
  61.6 0.9 copy-done.6
  62.5 0.9 copy-done.7
  63.4 1.9 %conv.1 = (f32[128,1024]{1,0:T(8,128)S(1)}, f32[1024,128]{1,0:T(8,128)S(1)}, f32[1024,128]{1,0:T(8,128)S(1)}, f32[128,128]{1,0:T(8,128)S(1)}, f32[8,32,128]{2,1,0:T(8,128)}) custom-call(bf16[128,1024]{1,0:T(8,128)(2,1)S(1)} %copy-done.6, bf16[3,1024]{1,0:T(4,128)(2,1)S(1)} %collective-permute-done.rim_ref, bf16[128,1024]{1,0:T(8,128)(2,1)S(1)} %copy-done.7, ...), custom_call_target="tpu_custom_call" | custom-call | flops 536870912 | bytes 4194304 | tf_op jit(solution)/shard_map/conv/pallas_call | solution.py:334
  65.3 0.8 copy-done.18
  66.1 0.8 copy-done.20
  66.9 0.8 copy-done.22
  67.7 0.6 copy-done.24
  68.4 0.0 all-to-all-done.4.got_ref
  68.4 6.5 %all-to-all-start = ((f32[8,32,128]{2,1,0:T(8,128)}), f32[8,32,128]{2,1,0:T(8,128)S(1)}, u32[]{:S(2)}, u32[]{:S(2)}) async-start(f32[8,32,128]{2,1,0:T(8,128)} %get-tuple-element.19), calls=%async_computation | async-start | bytes 262144 | tf_op jit(solution)/shard_map/all_to_all | solution.py:347
  74.9 2.0 %assemble_rest.1.refs_0_ = bf16[64,4096]{1,0:T(8,128)(2,1)} custom-call(bf16[64,8,512]{2,1,0:T(8,128)(2,1)} %all-to-all-done.4.got_ref), custom_call_target="tpu_custom_call" | custom-call | flops 268435456 | bytes 4194304 | tf_op jit(solution)/shard_map/assemble_rest/pallas_call | solution.py:80
  76.8 2.7 %collective-permute-start.3 = (bf16[64,4096]{1,0:T(8,128)(2,1)}, bf16[64,4096]{1,0:T(8,128)(2,1)}, u32[]{:S(2)}, u32[]{:S(2)}) collective-permute-start(bf16[64,4096]{1,0:T(8,128)(2,1)} %assemble_rest.1.refs_0_), channel_id=1, source_target_pairs={{0,16},{16,32},{32,48},{48,0},{1,17},{17,33},{33,49},{49,1},{2,18}... | collective-permute-start | bytes 1572872 | tf_op jit(solution)/shard_map/ppermute | solution.py:326
  79.5 4.5 %collective-permute-start.4 = (bf16[64,4096]{1,0:T(8,128)(2,1)}, bf16[64,4096]{1,0:T(8,128)(2,1)}, u32[]{:S(2)}, u32[]{:S(2)}) collective-permute-start(bf16[64,4096]{1,0:T(8,128)(2,1)} %assemble_rest.1.refs_0_), channel_id=1, source_target_pairs={{0,48},{16,0},{32,16},{48,32},{1,49},{17,1},{33,17},{49,33},{2,50}... | collective-permute-start | bytes 1572872 | tf_op jit(solution)/shard_map/ppermute | solution.py:327
  84.0 1.0 copy-done.21
  85.1 1.0 copy-done.23
  86.1 0.8 copy-done.25
  87.0 4.4 %scan.1 = (f32[1024,128]{1,0:T(8,128)S(1)}, f32[1024,128]{1,0:T(8,128)S(1)}, bf16[8,160,128]{2,1,0:T(8,128)(2,1)S(1)}) custom-call(f32[32,128]{1,0:T(8,128)S(1)} %reduce_sum.9.coef_ref, f32[1024,128]{1,0:T(8,128)S(1)} %copy-done.21, f32[1024,128]{1,0:T(8,128)S(1)} %copy-done.23, f32[128,128]{1,0:T(8,128)S(1)} %copy-done.25), custom_call_target="tpu_custom_call" | custom-call | flops 2147483648 | bytes 4194304 | tf_op jit(solution)/shard_map/scan/pallas_call | solution.py:349
  91.4 0.7 copy-done.5
  92.2 0.8 copy-done.30
  93.0 0.8 copy-done.32
  93.8 5.7 %all-to-all-start.1 = ((bf16[8,160,128]{2,1,0:T(8,128)(2,1)}), bf16[8,160,128]{2,1,0:T(8,128)(2,1)S(1)}, u32[]{:S(2)}, u32[]{:S(2)}) async-start(bf16[8,160,128]{2,1,0:T(8,128)(2,1)} %copy-done.5), calls=%async_computation.1 | async-start | bytes 655360 | tf_op jit(solution)/shard_map/all_to_all | solution.py:352
  99.5 0.0 collective-permute-done.3.refs_1_
  99.5 1.7 slice.12
  101.2 3.3 %collective-permute-start.5 = (bf16[32,4096]{1,0:T(8,128)(2,1)}, bf16[32,4096]{1,0:T(8,128)(2,1)}, u32[]{:S(2)}, u32[]{:S(2)}) collective-permute-start(bf16[32,4096]{1,0:T(8,128)(2,1)} %slice.12), channel_id=1, source_target_pairs={{0,16},{16,32},{32,48},{48,0},{1,17},{17,33},{33,49},{49,1},{2,18}... | collective-permute-start | bytes 786440 | tf_op jit(solution)/shard_map/ppermute | solution.py:328
  104.5 0.0 collective-permute-done.4.refs_2_
  104.5 1.7 slice.13
  106.2 3.2 %collective-permute-start.6 = (bf16[32,4096]{1,0:T(8,128)(2,1)}, bf16[32,4096]{1,0:T(8,128)(2,1)}, u32[]{:S(2)}, u32[]{:S(2)}) collective-permute-start(bf16[32,4096]{1,0:T(8,128)(2,1)} %slice.13), channel_id=1, source_target_pairs={{0,48},{16,0},{32,16},{48,32},{1,49},{17,1},{33,17},{49,33},{2,50}... | collective-permute-start | bytes 786440 | tf_op jit(solution)/shard_map/ppermute | solution.py:329
  109.4 0.2 group.1
  109.6 0.7 copy-done.4
  110.4 0.6 copy-done.28
  111.0 0.6 copy-done.34
  111.6 9.7 %all-to-all-start.2 = ((bf16[8,160,128]{2,1,0:T(8,128)(2,1)}), bf16[8,160,128]{2,1,0:T(8,128)(2,1)S(1)}, u32[]{:S(2)}, u32[]{:S(2)}) async-start(bf16[8,160,128]{2,1,0:T(8,128)(2,1)} %copy-done.4), calls=%async_computation.2 | async-start | bytes 655360 | tf_op jit(solution)/shard_map/all_to_all | solution.py:360
  121.3 11.5 %expand_rest.1 = (bf16[192,256]{1,0:T(8,128)(2,1)S(1)}, bf16[192,256]{1,0:T(8,128)(2,1)}) custom-call(bf16[192,4096]{1,0:T(8,128)(2,1)S(1)} %bitcast.10, bf16[192,4096]{1,0:T(8,128)(2,1)S(1)} %bitcast.13, bf16[192,4096]{1,0:T(8,128)(2,1)} %collective-permute-done.1.other_gate_ref, bf16[192,4096]{1,0:T(8,128)(2,1)} %collective-permute-done.2.other_up_ref, ...), custom_call_target="tpu_custom_call" | custom-call | flops 1610612736 | bytes 4194304 | tf_op jit(solution)/shard_map/expand_rest/pallas_call | solution.py:102
  132.8 0.6 copy-done.12
  133.5 3.0 %collective-permute-start.8 = (bf16[192,256]{1,0:T(8,128)(2,1)}, bf16[192,256]{1,0:T(8,128)(2,1)}, u32[]{:S(2)}, u32[]{:S(2)}) collective-permute-start(bf16[192,256]{1,0:T(8,128)(2,1)} %get-tuple-element.35), channel_id=1, source_target_pairs={{0,8},{8,0},{1,9},{9,1},{2,10},{10,2},{3,11},{11,3},{4,12},{12,4},... | collective-permute-start | bytes 294920 | tf_op jit(solution)/shard_map/ppermute | solution.py:372
  136.5 0.0 all-gather.2.cloned.1.call-done.refs_0_
  136.5 1.9 %copy-done.2 = bf16[384,4096]{1,0:T(8,128)(2,1)S(1)} copy-done((bf16[384,4096]{1,0:T(8,128)(2,1)S(1)}, bf16[384,4096]{1,0:T(8,128)(2,1)}, u32[]{:S(2)}) %copy-start.2) | copy-done | bytes 3145752
  138.4 6.7 %expand_first.1 = (bf16[192,384]{1,0:T(8,128)(2,1)S(1)}, bf16[192,384]{1,0:T(8,128)(2,1)}) custom-call(bf16[192,4096]{1,0:T(8,128)(2,1)S(1)} %bitcast.11, bf16[192,4096]{1,0:T(8,128)(2,1)S(1)} %bitcast.14, bf16[192,4096]{1,0:T(8,128)(2,1)} %collective-permute-done.1.other_gate_ref, bf16[192,4096]{1,0:T(8,128)(2,1)} %collective-permute-done.2.other_up_ref, ...), custom_call_target="tpu_custom_call" | custom-call | flops 2415919104 | bytes 4194304 | tf_op jit(solution)/shard_map/expand_first/pallas_call | solution.py:102
  145.1 0.7 copy-done.9
  145.7 1.9 %collective-permute-start.7 = (bf16[192,384]{1,0:T(8,128)(2,1)}, bf16[192,384]{1,0:T(8,128)(2,1)S(1)}, u32[]{:S(2)}, u32[]{:S(2)}) collective-permute-start(bf16[192,384]{1,0:T(8,128)(2,1)} %get-tuple-element.34), channel_id=1, source_target_pairs={{0,8},{8,0},{1,9},{9,1},{2,10},{10,2},{3,11},{11,3},{4,12},{12,4},... | collective-permute-start | bytes 442376 | tf_op jit(solution)/shard_map/ppermute | solution.py:373
  147.7 0.0 copy-start.8
  147.7 0.9 copy-done.8
  148.6 1.0 copy-done.19
  149.7 0.8 copy-done.27
  150.5 0.8 copy-done.29
  151.4 1.0 copy-done.31
  152.4 1.0 copy-done.33
  153.4 3.9 %finish.1 = bf16[128,1024]{1,0:T(8,128)(2,1)} custom-call(s32[1]{0:T(128)} %bitcast.mine_ref, f32[32,128]{1,0:T(8,128)S(1)} %reduce_sum.9.coef_ref, bf16[8,160,128]{2,1,0:T(8,128)(2,1)S(1)} %all-to-all-done.2.got_ref, f32[128,128]{1,0:T(8,128)S(1)} %copy-done.27, f32[128,128]{1,0:T(8,128)S(1)} %copy-done.29, f32[8,128]{1,0:T(8,128)S(1)} %copy-done.35, ...), custom_call_target="tpu_custom_call" | custom-call | flops 2147483648 | bytes 4194304 | tf_op jit(solution)/shard_map/finish/pallas_call | solution.py:362
  157.3 2.9 %order.1 = bf16[192,1280]{1,0:T(8,128)(2,1)} custom-call(s32[1]{0:T(128)} %bitcast.4.x_ref, s32[1]{0:T(128)} %bitcast.5.core_ref, bf16[192,384]{1,0:T(8,128)(2,1)S(1)} %copy-done.10, bf16[192,256]{1,0:T(8,128)(2,1)S(1)} %copy-done.13, bf16[192,384]{1,0:T(8,128)(2,1)S(1)} %collective-permute-done.7.other_first_ref, ...), custom_call_target="tpu_custom_call" | custom-call | flops 268435456 | bytes 4194304 | tf_op jit(solution)/shard_map/order/pallas_call | solution.py:376
  (54 shorter events, 0.1 us)
Async XLA Ops:
  7.2 129.3 %all-gather.2.cloned.1.call-start = ((), (), s32[]{:S(2)}) async-start(), calls=%async_computation.5 | async-start | bytes 3538944 | tf_op jit(solution)/shard_map/all_gather | solution.py:323
  8.0 0.9 copy-start.11
  9.4 0.9 copy-start.3
  10.3 40.2 %copy-start = (bf16[1,192,4096]{2,1,0:T(8,128)(2,1)S(1)}, bf16[1,192,4096]{2,1,0:T(8,128)(2,1)}, u32[]{:S(2)}) copy-start(bf16[1,192,4096]{2,1,0:T(8,128)(2,1)} %param.22) | copy-start | bytes 4718596
  10.3 45.0 %copy-start.1 = (bf16[1,192,4096]{2,1,0:T(8,128)(2,1)S(1)}, bf16[1,192,4096]{2,1,0:T(8,128)(2,1)}, u32[]{:S(2)}) copy-start(bf16[1,192,4096]{2,1,0:T(8,128)(2,1)} %param.23) | copy-start | bytes 4718596
  37.1 24.4 %copy-start.14 = (f32[16,1024]{1,0:T(8,128)S(1)}, f32[16,1024]{1,0:T(8,128)}, u32[]{:S(2)}) copy-start(f32[16,1024]{1,0:T(8,128)} %decay_ref.1) | copy-start | bytes 196612
  37.1 24.5 %copy-start.15 = (f32[4,1024]{1,0:T(4,128)S(1)}, f32[4,1024]{1,0:T(4,128)}, u32[]{:S(2)}) copy-start(f32[4,1024]{1,0:T(4,128)} %weight_ref.1) | copy-start | bytes 49156
  37.1 24.5 %copy-start.16 = (f32[1024]{0:T(1024)S(1)}, f32[1024]{0:T(1024)}, u32[]{:S(2)}) copy-start(f32[1024]{0:T(1024)} %param.17) | copy-start | bytes 12292
  37.9 30.4 %all-to-all-start.4 = ((bf16[64,8,512]{2,1,0:T(8,128)(2,1)}), bf16[64,8,512]{2,1,0:T(8,128)(2,1)}, u32[]{:S(2)}, u32[]{:S(2)}) async-start(bf16[64,8,512]{2,1,0:T(8,128)(2,1)} %copy-done.3), calls=%async_computation.4 | async-start | bytes 1048576 | tf_op jit(solution)/shard_map/all_to_all | solution.py:322
  50.5 70.8 %collective-permute-start.1 = (bf16[192,4096]{1,0:T(8,128)(2,1)S(1)}, bf16[192,4096]{1,0:T(8,128)(2,1)}, u32[]{:S(2)}, u32[]{:S(2)}) collective-permute-start(bf16[192,4096]{1,0:T(8,128)(2,1)S(1)} %bitcast.9), channel_id=1, source_target_pairs={{0,8},{8,0},{1,9},{9,1},{2,10},{10,2},{3,11},{11,3},{4,12},{12,4},... | collective-permute-start | bytes 4718600 | tf_op jit(solution)/shard_map/ppermute | solution.py:331
  55.3 66.0 %collective-permute-start.2 = (bf16[192,4096]{1,0:T(8,128)(2,1)S(1)}, bf16[192,4096]{1,0:T(8,128)(2,1)}, u32[]{:S(2)}, u32[]{:S(2)}) collective-permute-start(bf16[192,4096]{1,0:T(8,128)(2,1)S(1)} %bitcast.12), channel_id=1, source_target_pairs={{0,8},{8,0},{1,9},{9,1},{2,10},{10,2},{3,11},{11,3},{4,12},{12,4},... | collective-permute-start | bytes 4718600 | tf_op jit(solution)/shard_map/ppermute | solution.py:331
  58.0 3.5 %collective-permute-start = (bf16[3,1024]{1,0:T(4,128)(2,1)S(1)}, bf16[3,1024]{1,0:T(4,128)(2,1)S(1)}, u32[]{:S(2)}, u32[]{:S(2)}) collective-permute-start(bf16[3,1024]{1,0:T(4,128)(2,1)S(1)} %slice.9), channel_id=1, source_target_pairs={{0,8},{8,16},{16,24},{24,32},{32,40},{40,48},{48,56},{56,64},{64,7... | collective-permute-start | bytes 18440 | tf_op jit(solution)/shard_map/ppermute | solution.py:311
  61.5 1.0 copy-start.6
  62.5 0.9 copy-start.7
  65.3 0.8 copy-start.18
  66.1 0.8 copy-start.20
  66.9 0.8 copy-start.22
  67.7 0.6 copy-start.24
  68.4 15.6 %all-to-all-start = ((f32[8,32,128]{2,1,0:T(8,128)}), f32[8,32,128]{2,1,0:T(8,128)S(1)}, u32[]{:S(2)}, u32[]{:S(2)}) async-start(f32[8,32,128]{2,1,0:T(8,128)} %get-tuple-element.19), calls=%async_computation | async-start | bytes 262144 | tf_op jit(solution)/shard_map/all_to_all | solution.py:347
  76.8 22.7 %collective-permute-start.3 = (bf16[64,4096]{1,0:T(8,128)(2,1)}, bf16[64,4096]{1,0:T(8,128)(2,1)}, u32[]{:S(2)}, u32[]{:S(2)}) collective-permute-start(bf16[64,4096]{1,0:T(8,128)(2,1)} %assemble_rest.1.refs_0_), channel_id=1, source_target_pairs={{0,16},{16,32},{32,48},{48,0},{1,17},{17,33},{33,49},{49,1},{2,18}... | collective-permute-start | bytes 1572872 | tf_op jit(solution)/shard_map/ppermute | solution.py:326
  79.5 25.0 %collective-permute-start.4 = (bf16[64,4096]{1,0:T(8,128)(2,1)}, bf16[64,4096]{1,0:T(8,128)(2,1)}, u32[]{:S(2)}, u32[]{:S(2)}) collective-permute-start(bf16[64,4096]{1,0:T(8,128)(2,1)} %assemble_rest.1.refs_0_), channel_id=1, source_target_pairs={{0,48},{16,0},{32,16},{48,32},{1,49},{17,1},{33,17},{49,33},{2,50}... | collective-permute-start | bytes 1572872 | tf_op jit(solution)/shard_map/ppermute | solution.py:327
  84.0 1.0 copy-start.21
  85.1 1.0 copy-start.23
  86.1 0.8 copy-start.25
  91.4 0.7 copy-start.5
  92.2 0.8 copy-start.30
  92.9 0.8 copy-start.32
  93.8 15.6 %copy-start.26 = (f32[128,128]{1,0:T(8,128)S(1)}, f32[128,128]{1,0:T(8,128)}, u32[]{:S(2)}) copy-start(f32[128,128]{1,0:T(8,128)} %copy-done.24) | copy-start | bytes 196612
  93.8 15.6 %all-to-all-start.1 = ((bf16[8,160,128]{2,1,0:T(8,128)(2,1)}), bf16[8,160,128]{2,1,0:T(8,128)(2,1)S(1)}, u32[]{:S(2)}, u32[]{:S(2)}) async-start(bf16[8,160,128]{2,1,0:T(8,128)(2,1)} %copy-done.5), calls=%async_computation.1 | async-start | bytes 655360 | tf_op jit(solution)/shard_map/all_to_all | solution.py:352
  101.2 20.1 %collective-permute-start.5 = (bf16[32,4096]{1,0:T(8,128)(2,1)}, bf16[32,4096]{1,0:T(8,128)(2,1)}, u32[]{:S(2)}, u32[]{:S(2)}) collective-permute-start(bf16[32,4096]{1,0:T(8,128)(2,1)} %slice.12), channel_id=1, source_target_pairs={{0,16},{16,32},{32,48},{48,0},{1,17},{17,33},{33,49},{49,1},{2,18}... | collective-permute-start | bytes 786440 | tf_op jit(solution)/shard_map/ppermute | solution.py:328
  106.2 15.2 %collective-permute-start.6 = (bf16[32,4096]{1,0:T(8,128)(2,1)}, bf16[32,4096]{1,0:T(8,128)(2,1)}, u32[]{:S(2)}, u32[]{:S(2)}) collective-permute-start(bf16[32,4096]{1,0:T(8,128)(2,1)} %slice.13), channel_id=1, source_target_pairs={{0,48},{16,0},{32,16},{48,32},{1,49},{17,1},{33,17},{49,33},{2,50}... | collective-permute-start | bytes 786440 | tf_op jit(solution)/shard_map/ppermute | solution.py:329
  109.6 0.7 copy-start.4
  110.4 0.6 copy-start.28
  111.0 0.6 copy-start.34
  111.6 36.1 %all-to-all-start.2 = ((bf16[8,160,128]{2,1,0:T(8,128)(2,1)}), bf16[8,160,128]{2,1,0:T(8,128)(2,1)S(1)}, u32[]{:S(2)}, u32[]{:S(2)}) async-start(bf16[8,160,128]{2,1,0:T(8,128)(2,1)} %copy-done.4), calls=%async_computation.2 | async-start | bytes 655360 | tf_op jit(solution)/shard_map/all_to_all | solution.py:360
  132.8 0.6 copy-start.12
  133.5 23.9 %collective-permute-start.8 = (bf16[192,256]{1,0:T(8,128)(2,1)}, bf16[192,256]{1,0:T(8,128)(2,1)}, u32[]{:S(2)}, u32[]{:S(2)}) collective-permute-start(bf16[192,256]{1,0:T(8,128)(2,1)} %get-tuple-element.35), channel_id=1, source_target_pairs={{0,8},{8,0},{1,9},{9,1},{2,10},{10,2},{3,11},{11,3},{4,12},{12,4},... | collective-permute-start | bytes 294920 | tf_op jit(solution)/shard_map/ppermute | solution.py:372
  136.5 1.9 %copy-start.2 = (bf16[384,4096]{1,0:T(8,128)(2,1)S(1)}, bf16[384,4096]{1,0:T(8,128)(2,1)}, u32[]{:S(2)}) copy-start(bf16[384,4096]{1,0:T(8,128)(2,1)} %all-gather.2.cloned.1.call-done.refs_0_) | copy-start | bytes 9437188
  138.4 9.3 %copy-start.17 = (f32[1024]{0:T(1024)S(1)}, f32[1024]{0:T(1024)}, u32[]{:S(2)}) copy-start(f32[1024]{0:T(1024)} %param.19) | copy-start | bytes 12292
  138.4 9.3 %copy-start.35 = (f32[8,128]{1,0:T(8,128)S(1)}, f32[8,128]{1,0:T(8,128)}, u32[]{:S(2)}) copy-start(f32[8,128]{1,0:T(8,128)} %copy-done.34) | copy-start | bytes 12292
  145.1 0.7 copy-start.9
  145.7 11.6 %collective-permute-start.7 = (bf16[192,384]{1,0:T(8,128)(2,1)}, bf16[192,384]{1,0:T(8,128)(2,1)S(1)}, u32[]{:S(2)}, u32[]{:S(2)}) collective-permute-start(bf16[192,384]{1,0:T(8,128)(2,1)} %get-tuple-element.34), channel_id=1, source_target_pairs={{0,8},{8,0},{1,9},{9,1},{2,10},{10,2},{3,11},{11,3},{4,12},{12,4},... | collective-permute-start | bytes 442376 | tf_op jit(solution)/shard_map/ppermute | solution.py:373
  147.7 1.0 copy-start.8
  148.6 1.0 copy-start.19
  149.7 0.8 copy-start.27
  150.5 0.8 copy-start.29
  151.4 1.0 copy-start.31
  152.4 1.0 copy-start.33
  153.4 3.9 %copy-start.10 = (bf16[192,384]{1,0:T(8,128)(2,1)S(1)}, bf16[192,384]{1,0:T(8,128)(2,1)}, u32[]{:S(2)}) copy-start(bf16[192,384]{1,0:T(8,128)(2,1)} %copy-done.9) | copy-start | bytes 442372
  153.4 3.9 %copy-start.13 = (bf16[192,256]{1,0:T(8,128)(2,1)S(1)}, bf16[192,256]{1,0:T(8,128)(2,1)}, u32[]{:S(2)}) copy-start(bf16[192,256]{1,0:T(8,128)(2,1)} %copy-done.12) | copy-start | bytes 294916
Sparse Core Ops, SparseCore 0:
  38.1 58.8 all-gather.1

commit v3 on v1

--- a/solution.py
+++ b/solution.py
@@ -14,20 +14,73 @@
 LOG2E = 1.4426950408889634
 SEQ = ("z", "x", "c")
 
+FIRST = 12
+REST = CAP - FIRST
+
 VMEM = pl.BlockSpec(memory_space=pltpu.VMEM)
 SMEM = pl.BlockSpec(memory_space=pltpu.SMEM)
-
-
-def call(kernel, out_shape, in_specs, scratch=(), name=None):
-    return pl.pallas_call(
-        kernel,
-        out_shape=out_shape,
-        in_specs=in_specs,
-        out_specs=jax.tree.map(lambda _: VMEM, out_shape),
-        scratch_shapes=scratch,
-        name=name,
-        compiler_params=pltpu.CompilerParams(vmem_limit_bytes=48 << 20),
-    )
+WHOLE = pl.BlockSpec(memory_space=pltpu.HBM)
+
+
+def call(kernel, out_shape, in_specs, scratch=(), name=None, vmem=60, flops=0, lazy=False, stack=0):
+    single = not isinstance(out_shape, tuple)
+    outs = (out_shape,) if single else out_shape
+
+    def run(*operands):
+        moved = [index for index in range(stack, len(in_specs)) if in_specs[index] is WHOLE]
+        buffers = [pltpu.VMEM(operands[index].shape, operands[index].dtype) for index in moved]
+        buffers += [pltpu.VMEM(out.shape, out.dtype) for out in outs]
+        sizes = [operand.shape[0] for operand in operands[:stack]]
+        if stack:
+            buffers.append(pltpu.VMEM((sum(sizes),) + operands[0].shape[1:], operands[0].dtype))
+        count = len(operands)
+
+        def body(*refs):
+            inputs, results = list(refs[:count]), refs[count : count + len(outs)]
+            held = refs[count + len(outs) : count + len(outs) + len(buffers)]
+            rest, sems = refs[count + len(outs) + len(buffers) : -1], refs[-1]
+            copies = []
+            for place, index in enumerate(moved):
+                copies.append(pltpu.make_async_copy(inputs[index], held[place], sems.at[place]))
+                inputs[index] = held[place]
+            for place, size in enumerate(sizes):
+                target = held[-1].at[pl.ds(sum(sizes[:place]), size)]
+                copies.append(
+                    pltpu.make_async_copy(inputs[place], target, sems.at[len(buffers) + place])
+                )
+            for copy in copies:
+                copy.start()
+            if stack:
+                inputs = [held[-1]] + inputs[stack:]
+            made = held[len(moved) : len(moved) + len(outs)]
+            if lazy:
+                kernel(copies, *inputs, *made, *rest)
+            else:
+                for copy in copies:
+                    copy.wait()
+                kernel(*inputs, *made, *rest)
+            copies = [
+                pltpu.make_async_copy(source, target, sems.at[len(moved) + place])
+                for place, (source, target) in enumerate(zip(made, results))
+            ]
+            for copy in copies:
+                copy.start()
+            for copy in copies:
+                copy.wait()
+
+        found = pl.pallas_call(
+            body,
+            out_shape=outs,
+            in_specs=in_specs,
+            out_specs=(WHOLE,) * len(outs),
+            scratch_shapes=[*buffers, *scratch, pltpu.SemaphoreType.DMA((len(buffers) + stack,))],
+            name=name,
+            compiler_params=pltpu.CompilerParams(vmem_limit_bytes=vmem << 20),
+            cost_estimate=pl.CostEstimate(flops=flops, transcendentals=0, bytes_accessed=4 << 20),
+        )(*operands)
+        return found[0] if single else found
+
+    return run
 
 
 def shape(dims, dtype):
@@ -53,6 +106,76 @@
     ).astype(BF16)
     for index in range(8):
         out_ref[index] = placed[index * 32 : index * 32 + CAP]
+
+
+def unpack_kernel(got_ref, first_ref, rest_ref, wide):
+    for block in range(8):
+        wide[:, block * 512 : block * 512 + 512] = got_ref[block].astype(F32)
+    first_ref[...] = wide[:FIRST].astype(BF16)
+    rest = wide[FIRST:].astype(BF16)
+    for copy in range(8):
+        rest_ref[copy] = rest
+
+
+def join_kernel(*refs):
+    parts, out_ref, wide = refs[:-2], refs[-2], refs[-1]
+    for index, ref in enumerate(parts):
+        wide[index * FIRST : index * FIRST + FIRST, :] = ref[...].astype(F32)
+    out_ref[...] = wide[...].astype(BF16)
+
+
+def expand_kernel(copies, rows_ref, other_ref, weight_ref, other_out_ref, out_ref):
+    dims = (((1,), (1,)), ((), ()))
+    units = out_ref.shape[0]
+    for copy in copies[2:]:
+        copy.wait()
+    sets = ((copies[0], other_ref, other_out_ref), (copies[1], weight_ref, out_ref))
+    for copy, weight, out in sets:
+        copy.wait()
+        both = lax.dot_general(weight[...], rows_ref[...], dims, preferred_element_type=F32)
+        out[...] = (silu(both[:units]) * both[units:]).astype(BF16)
+
+
+def expand(weights, blocks, name):
+    units, count = weights[0].shape[0] // 2, sum(block.shape[0] for block in blocks)
+    return call(
+        expand_kernel,
+        (shape((units, count), BF16),) * 2,
+        [WHOLE] * (2 + len(blocks)),
+        name=name,
+        flops=8 * units * count * 4096,
+        lazy=True,
+        stack=len(blocks),
+    )(*blocks, weights[1], weights[0])
+
+
+def divided(value, by):
+    return (value * (65536 // by + 1)) >> 16
+
+
+def order_kernel(x_ref, core_ref, first_ref, rest_ref, other_first_ref, other_rest_ref, out_ref):
+    columns = out_ref.shape[1]
+    total = jnp.zeros(out_ref.shape, F32)
+    sets = ((first_ref, rest_ref, core_ref[0]), (other_first_ref, other_rest_ref, 1 - core_ref[0]))
+    for early_ref, late_ref, core in sets:
+        for ref in (early_ref, late_ref):
+            count = ref.shape[1]
+            row = lax.broadcasted_iota(jnp.int32, (count, 1), 0)
+            if ref is early_ref:
+                block = divided(row, FIRST)
+                slot = row - block * FIRST
+                layer, near = block >> 2, block & 3
+            else:
+                block = divided(row, REST)
+                slot = row - block * REST + FIRST
+                layer, near = block & 7, block >> 3
+            across = (x_ref[0] + jnp.where(near == 0, 0, jnp.where(near == 1, 3, near - 1))) & 3
+            column = ((layer * 4 + across) * 2 + core) * CAP + slot
+            table = lax.broadcasted_iota(jnp.int32, (count, columns), 1) == column
+            total = total + jnp.dot(
+                ref[...], jnp.where(table, 1.0, 0.0).astype(BF16), preferred_element_type=F32
+            )
+    out_ref[...] = total.astype(BF16)
 
 
 def silu(value):
@@ -214,13 +337,6 @@
         out_ref[:, lanes] = (value * silu(z_ref[:, lanes].astype(F32))).astype(BF16)
 
 
-def expand_rows(slot_rows, gate_matrix, up_matrix):
-    dims = (((1,), (1,)), ((), ()))
-    gate_part = lax.dot_general(gate_matrix, slot_rows, dims, preferred_element_type=F32)
-    up_part = lax.dot_general(up_matrix, slot_rows, dims, preferred_element_type=F32)
-    return (jax.nn.silu(gate_part) * up_part).astype(BF16)
-
-
 def shards(
     inner_x,
     inner_z,
@@ -238,11 +354,14 @@
     rows, width = inner_x.shape
     shards_of = lax.axis_size(SEQ)
     rim = lax.ppermute(inner_x[rows - 3 :], SEQ, [(i, i + 1) for i in range(shards_of - 1)])
-    placed = call(place_kernel, shape((8, CAP, moe_tokens.shape[1]), BF16), [VMEM] * 2, name="place")(
-        routes, moe_tokens
-    )
-    arrived = lax.all_to_all(placed, "exp", split_axis=0, concat_axis=2, tiled=True)
-    gathered = lax.all_gather(arrived[0], SEQ, axis=0, tiled=True)
+    swap = [(0, 1), (1, 0)]
+    features = moe_tokens.shape[1]
+    placed = call(
+        place_kernel, shape((8, CAP, features), BF16), [WHOLE] * 2, name="place", flops=1 << 28
+    )(routes, moe_tokens)
+    arrived = lax.all_to_all(placed, "exp", split_axis=0, concat_axis=0, tiled=True)
+    weight = jnp.concatenate([gate_weight[0], up_weight[0]], axis=0)
+    weights = [weight, lax.ppermute(weight, "c", swap)]
 
     dense = shape((rows * width // 128, 128), F32)
     conv, step, drive, rate, part = call(
@@ -254,34 +373,76 @@
             shape((128, 128), F32),
             shape((8, 32, rows), F32),
         ),
-        [VMEM] * 7,
+        [WHOLE] * 7,
         [pltpu.VMEM((rows + 8, width), F32)],
-        name="conv",
+        name="conv", flops=1 << 29,
     )(inner_x, rim, step_raw, conv_weight, state_proj, step_bias[None], decay_log)
+    arrived, _, _ = lax.optimization_barrier((arrived, part, weight))
+    first, rest = call(
+        unpack_kernel,
+        (shape((FIRST, 4096), BF16), shape((8, REST, 4096), BF16)),
+        [WHOLE],
+        [pltpu.VMEM((CAP, 4096), F32)],
+        name="unpack",
+        vmem=16,
+        flops=1 << 28,
+    )(arrived)
+    shifted = [
+        lax.ppermute(first, "x", [(i, (i + step) % 4) for i in range(4)]) for step in (1, 3, 2)
+    ]
+    first = call(
+        join_kernel,
+        shape((4 * FIRST, 4096), BF16),
+        [WHOLE] * 4,
+        [pltpu.VMEM((4 * FIRST, 4096), F32)],
+        name="join",
+        flops=1 << 28,
+    )(first, *shifted)
+    first = lax.all_gather(first, "z", axis=0, tiled=True)
     coef = jnp.sum(lax.all_to_all(part, "exp", split_axis=0, concat_axis=0, tiled=True), axis=0)
+    rest, coef = lax.optimization_barrier((rest, coef))
+    rest = lax.all_to_all(rest, "z", split_axis=0, concat_axis=0, tiled=True).reshape(-1, 4096)
+    half = rest.shape[0] // 2
+    ahead, back = ([(i, (i + step) % 4) for i in range(4)] for step in (1, 3))
+    left, right = lax.ppermute(rest, "x", ahead), lax.ppermute(rest, "x", back)
+    far_left = lax.ppermute(left[:half], "x", ahead)
+    far_right = lax.ppermute(right[half:], "x", back)
     packed = shape((8, 160, 128), BF16)
     local, sums, ends = call(
-        scan_kernel, (dense, dense, packed), [SMEM] + [VMEM] * 3, name="scan"
+        scan_kernel, (dense, dense, packed), [SMEM] + [WHOLE] * 3, name="scan", flops=1 << 31
     )(coef, step, drive, rate)
+    ends, _ = lax.optimization_barrier((ends, rest))
     near = lax.all_to_all(ends, ("x", "c"), split_axis=0, concat_axis=0, tiled=True)
     place_in = lax.axis_index(("x", "c")).astype(jnp.int32).reshape(1)
     before, before_step, whole = call(
         group_kernel,
         (shape((128, 128), F32), shape((8, 128), F32), packed),
-        [SMEM, VMEM, VMEM],
-        name="group",
+        [SMEM, WHOLE, WHOLE],
+        name="group", vmem=16, flops=1 << 28,
     )(place_in, near, rate)
     far = lax.all_to_all(whole, "z", split_axis=0, concat_axis=0, tiled=True)
     layer = lax.axis_index("z").astype(jnp.int32).reshape(1)
     mixed = call(
         finish_kernel,
         shape((rows, width), BF16),
-        [SMEM, SMEM] + [VMEM] * 9,
+        [SMEM, SMEM] + [WHOLE] * 9,
         [pltpu.VMEM(dense.shape, F32)],
-        name="finish",
+        name="finish", flops=1 << 31,
     )(layer, coef, far, rate, before, before_step, local, sums, conv, skip_gain[None], inner_z)
 
-    hidden = expand_rows(gathered, gate_weight[0], up_weight[0])[None]
+    theirs_rest, mine_rest = expand(weights, [rest, left, right, far_left, far_right], "expand_rest")
+    theirs, mine = expand(weights, [first], "expand_first")
+    other_rest = lax.ppermute(theirs_rest, "c", swap)
+    other = lax.ppermute(theirs, "c", swap)
+    here = [lax.axis_index(axis).astype(jnp.int32).reshape(1) for axis in ("x", "c")]
+    units = gate_weight.shape[1]
+    hidden = call(
+        order_kernel,
+        shape((units, 1280), BF16),
+        [SMEM] * 2 + [WHOLE] * 4,
+        name="order",
+        flops=1 << 28,
+    )(*here, mine, mine_rest, other, other_rest)[None]
     return mixed, hidden
 
 

time: 160 us -> 175 us (1.094)
  waiting for transfers between devices: 42.3 us -> 6.22 us
  Pallas kernels: 11.6 us -> 41 us
  starting transfers between devices: 24.2 us -> 52.5 us
  blocking collectives: 26.8 us -> 47.3 us
  local copies, waits for them, and re-layouts: 27.8 us -> 7.61 us
  matrix products: 12.1 us -> 0 us
  other arithmetic: 0.01 us -> 4.51 us
    ppermute x0 -> x10, starting transfers between devices: none -> 31.1 us  [the longest x3 10.2 us: shards(): lax.ppermute(first, 'x', [(i, (i + step) % 4) for i in range(4)])]
    pallas_call x5 -> x10, Pallas kernels: 11.6 us -> 41 us  [run(): pl.pallas_call(body, out_shape=outs, in_specs=in_specs, out_specs=(WHOLE,...]
    unnamed x34 -> x36, local copies, waits for them, and re-layouts: 27.1 us -> 6.84 us
    all_gather x1, waiting for transfers between devices: 18.8 us -> 0.02 us  [shards(): first = lax.all_gather(first, 'z', axis=0, tiled=True)]
    all_to_all x1, waiting for transfers between devices: 16.4 us -> 0.01 us  [shards(): far = lax.all_to_all(whole, 'z', split_axis=0, concat_axis=0, tiled=True)]
    all_to_all x1, blocking collectives: 16.2 us -> 31.9 us  [shards(): lax.all_to_all(rest, 'z', split_axis=0, concat_axis=0, tiled=True)]
    dot_general x2 -> x0, matrix products: 12.1 us -> none  [the longest x1 7.72 us: expand_rows(): lax.dot_general(gate_matrix, slot_rows, dims, preferred_element_type=F32)]
    all_to_all x1, starting transfers between devices: 11.9 us -> 3.43 us  [shards(): far = lax.all_to_all(whole, 'z', split_axis=0, concat_axis=0, tiled=True)]
  transfers between devices with their start and end apart: 4 -> 15, of which waited for: 3 -> 3; matrix products, arithmetic and copies ran while one was open for 1% -> 4% of each run, Pallas kernels for 7% -> 19%
where the time goes in v3:
time: 175 us; the launch traced here: 174 us
  starting transfers between devices  52.5 us (30%)
  blocking collectives  47.3 us (27%)
  Pallas kernels  41 us (23%)
  between operations  14.5 us (8%)
  local copies, waits for them, and re-layouts  7.61 us (4%)
  waiting for transfers between devices  6.22 us (4%)
  other arithmetic  4.51 us (3%)
    pallas_call x10, Pallas kernels, run(): pl.pallas_call(body, out_shape=outs, in_specs=in_specs, out_specs=(WHOLE,...  41 us
    all_to_all x1, blocking collectives, shards(): lax.all_to_all(rest, 'z', split_axis=0, concat_axis=0, tiled=True)  31.9 us
    all_to_all x1, blocking collectives, shards(): lax.all_to_all(part, 'exp', split_axis=0, concat_axis=0, tiled=True)  15.4 us
    ppermute x3, starting transfers between devices, shards(): lax.ppermute(first, 'x', [(i, (i + step) % 4) for i in range(4)])  10.2 us
    all_to_all x1, starting transfers between devices, shards(): lax.all_to_all(placed, 'exp', split_axis=0, concat_axis=0, tiled=True)  7.66 us
    unnamed x36, local copies, waits for them, and re-layouts  6.84 us
    all_to_all x1, starting transfers between devices, shards(): lax.all_to_all(ends, ('x', 'c'), split_axis=0, concat_axis=0, tiled=True)  6.32 us
    ppermute x3, waiting for transfers between devices, shards(): lax.ppermute(first, 'x', [(i, (i + step) % 4) for i in range(4)])  5.52 us
  transfers between devices with their start and end apart: 15, of which 3 were waited for; matrix products, arithmetic and copies ran while one was open for 4% of the time, Pallas kernels for 19%

profile of v3, /device:TPU:1, one launch (start us, length us, event | category | flops | bytes accessed | tf_op | source)
XLA Modules:
  0.0 173.6 jit_solution(11378533075751112034)
XLA Ops:
  7.2 1.4 copy.14.refs_0_
  8.6 2.1 %place.1 = bf16[8,20,512]{2,1,0:T(8,128)(2,1)} custom-call(s32[128,2]{1,0:T(8,128)} %copy.14.refs_0_, bf16[128,512]{1,0:T(8,128)(2,1)} %refs_1_.1), custom_call_target="tpu_custom_call" | custom-call | flops 268435456 | bytes 4194304 | tf_op jit(solution)/shard_map/place/pallas_call | solution.py:71
  10.7 7.7 %all-to-all-start = ((bf16[8,20,512]{2,1,0:T(8,128)(2,1)}), bf16[8,20,512]{2,1,0:T(8,128)(2,1)S(1)}, u32[]{:S(2)}, u32[]{:S(2)}) async-start(bf16[8,20,512]{2,1,0:T(8,128)(2,1)} %place.1), calls=%async_computation | async-start | bytes 393216 | tf_op jit(solution)/shard_map/all_to_all | solution.py:362
  18.4 0.0 all-gather.2.cloned.1.call-start
  18.4 0.7 slice.9
  19.2 3.9 %collective-permute-start = (bf16[3,1024]{1,0:T(4,128)(2,1)S(1)}, bf16[3,1024]{1,0:T(4,128)(2,1)S(1)}, u32[]{:S(2)}, u32[]{:S(2)}) collective-permute-start(bf16[3,1024]{1,0:T(4,128)(2,1)S(1)} %slice.9), channel_id=1, source_target_pairs={{0,8},{8,16},{16,24},{24,32},{32,40},{40,48},{48,56},{56,64},{64,7... | collective-permute-start | bytes 18440 | tf_op jit(solution)/shard_map/ppermute | solution.py:356
  23.1 0.0 copy-start.10
  23.1 3.9 %pad_maximum_fusion.refs_2_.refs_6_ = bf16[384,4096]{1,0:T(8,128)(2,1)} fusion(bf16[192,4096]{1,0:T(8,128)(2,1)} %bitcast.13, bf16[192,4096]{1,0:T(8,128)(2,1)} %bitcast.14), kind=kLoop, calls=%fused_computation | loop fusion | flops 6291456 | bytes 6291456 | tf_op jit(solution)/shard_map/concatenate | solution.py:363
  27.0 0.0 copy-done.10
  27.0 0.8 copy.15.refs_4_
  27.9 0.0 collective-permute-done.refs_1_
  27.9 0.6 copy-done.16
  28.5 3.5 %conv.1 = (f32[128,1024]{1,0:T(8,128)}, f32[1024,128]{1,0:T(8,128)}, f32[1024,128]{1,0:T(8,128)}, f32[128,128]{1,0:T(8,128)}, f32[8,32,128]{2,1,0:T(8,128)}) custom-call(bf16[128,1024]{1,0:T(8,128)(2,1)} %refs_0_.2, bf16[3,1024]{1,0:T(4,128)(2,1)} %copy-done.16, bf16[128,1024]{1,0:T(8,128)(2,1)} %refs_2_.1, f32[4,1024]{1,0:T(4,128)} %refs_3_.1, ...), custom_call_target="tpu_custom_call" | custom-call | flops 536870912 | bytes 4194304 | tf_op jit(solution)/shard_map/conv/pallas_call | solution.py:71
  32.0 0.0 all-to-all-done.refs_0_
  32.0 0.6 unpack.1
  32.6 0.0 copy-start
  32.6 3.1 %collective-permute-start.1 = (bf16[12,4096]{1,0:T(8,128)(2,1)S(1)}, bf16[12,4096]{1,0:T(8,128)(2,1)S(1)}, u32[]{:S(2)}, u32[]{:S(2)}) collective-permute-start(bf16[12,4096]{1,0:T(8,128)(2,1)S(1)} %get-tuple-element.39.refs_0_), channel_id=1, source_target_pairs={{0,16},{16,32},{32,48},{48,0},{1,17},{17,33},{33,49},{49,1},{2,18}... | collective-permute-start | bytes 294920 | tf_op jit(solution)/shard_map/ppermute | solution.py:391
  35.7 4.0 %collective-permute-start.2 = (bf16[12,4096]{1,0:T(8,128)(2,1)S(1)}, bf16[12,4096]{1,0:T(8,128)(2,1)S(1)}, u32[]{:S(2)}, u32[]{:S(2)}) collective-permute-start(bf16[12,4096]{1,0:T(8,128)(2,1)S(1)} %get-tuple-element.39.refs_0_), channel_id=1, source_target_pairs={{0,48},{16,0},{32,16},{48,32},{1,49},{17,1},{33,17},{49,33},{2,50}... | collective-permute-start | bytes 294920 | tf_op jit(solution)/shard_map/ppermute | solution.py:391
  39.7 3.1 %collective-permute-start.3 = (bf16[12,4096]{1,0:T(8,128)(2,1)S(1)}, bf16[12,4096]{1,0:T(8,128)(2,1)S(1)}, u32[]{:S(2)}, u32[]{:S(2)}) collective-permute-start(bf16[12,4096]{1,0:T(8,128)(2,1)S(1)} %get-tuple-element.39.refs_0_), channel_id=1, source_target_pairs={{0,32},{16,48},{32,0},{48,16},{1,33},{17,49},{33,1},{49,17},{2,34}... | collective-permute-start | bytes 294920 | tf_op jit(solution)/shard_map/ppermute | solution.py:391
  42.8 0.0 collective-permute-done.1.refs_1_
  42.8 0.0 copy-start.12
  42.8 0.1 collective-permute-done.2.refs_2_
  42.9 5.4 %collective-permute-done.3.refs_3_ = bf16[12,4096]{1,0:T(8,128)(2,1)S(1)} collective-permute-done((bf16[12,4096]{1,0:T(8,128)(2,1)S(1)}, bf16[12,4096]{1,0:T(8,128)(2,1)S(1)}, u32[]{:S(2)}, u32[]{:S(2)}) %collective-permute-start.3) | collective-permute-done | bytes 98336 | tf_op jit(solution)/shard_map/ppermute | solution.py:391
  48.4 0.0 copy-done.12
  48.4 0.6 copy-done.14
  49.0 2.0 %join.1 = bf16[48,4096]{1,0:T(8,128)(2,1)} custom-call(bf16[12,4096]{1,0:T(8,128)(2,1)} %copy-done, bf16[12,4096]{1,0:T(8,128)(2,1)} %copy-done.12, bf16[12,4096]{1,0:T(8,128)(2,1)} %copy-done.13, bf16[12,4096]{1,0:T(8,128)(2,1)} %copy-done.14), custom_call_target="tpu_custom_call" | custom-call | flops 268435456 | bytes 4194304 | tf_op jit(solution)/shard_map/join/pallas_call | solution.py:71
  51.0 0.0 all-gather.2.cloned.1.call-update
  51.0 2.6 %collective-permute-start.4 = (bf16[384,4096]{1,0:T(8,128)(2,1)}, bf16[384,4096]{1,0:T(8,128)(2,1)}, u32[]{:S(2)}, u32[]{:S(2)}) collective-permute-start(bf16[384,4096]{1,0:T(8,128)(2,1)} %pad_maximum_fusion.refs_2_.refs_6_), channel_id=1, source_target_pairs={{0,8},{8,0},{1,9},{9,1},{2,10},{10,2},{3,11},{11,3},{4,12},{12,4},... | collective-permute-start | bytes 9437192 | tf_op jit(solution)/shard_map/ppermute | solution.py:364
  53.6 15.4 %all_to_all.25 = f32[8,32,128]{2,1,0:T(8,128)S(1)} all-to-all(f32[8,32,128]{2,1,0:T(8,128)} %get-tuple-element.23), channel_id=1, replica_groups=mesh['z'=8,'x'=4,'c'=2,'exp'=8] {'exp'}, dimensions={0} | all-to-all | bytes 262144 | tf_op jit(solution)/shard_map/all_to_all | solution.py:402
  69.0 0.6 reduce_sum.9.refs_0_.refs_1_
  69.6 31.9 %all_to_all.26 = bf16[8,8,4096]{2,1,0:T(8,128)(2,1)S(1)} all-to-all(bf16[8,8,4096]{2,1,0:T(8,128)(2,1)S(1)} %get-tuple-element.31), channel_id=1, replica_groups=mesh['z'=8,'x'=4,'c'=2,'exp'=8] {'z'}, dimensions={0} | all-to-all | bytes 1048576 | tf_op jit(solution)/shard_map/all_to_all | solution.py:404
  101.5 1.9 %collective-permute-start.5 = (bf16[64,4096]{1,0:T(8,128)(2,1)S(1)}, bf16[64,4096]{1,0:T(8,128)(2,1)S(1)}, u32[]{:S(2)}, u32[]{:S(2)}) collective-permute-start(bf16[64,4096]{1,0:T(8,128)(2,1)S(1)} %bitcast.10), channel_id=1, source_target_pairs={{0,16},{16,32},{32,48},{48,0},{1,17},{17,33},{33,49},{49,1},{2,18}... | collective-permute-start | bytes 1572872 | tf_op jit(solution)/shard_map/ppermute | solution.py:407
  103.4 4.6 %collective-permute-start.6 = (bf16[64,4096]{1,0:T(8,128)(2,1)S(1)}, bf16[64,4096]{1,0:T(8,128)(2,1)S(1)}, u32[]{:S(2)}, u32[]{:S(2)}) collective-permute-start(bf16[64,4096]{1,0:T(8,128)(2,1)S(1)} %bitcast.11), channel_id=1, source_target_pairs={{0,48},{16,0},{32,16},{48,32},{1,49},{17,1},{33,17},{49,33},{2,50}... | collective-permute-start | bytes 1572872 | tf_op jit(solution)/shard_map/ppermute | solution.py:407
  108.0 7.0 %scan.1 = (f32[1024,128]{1,0:T(8,128)}, f32[1024,128]{1,0:T(8,128)}, bf16[8,160,128]{2,1,0:T(8,128)(2,1)}) custom-call(f32[32,128]{1,0:T(8,128)} %reduce_sum.9.refs_0_.refs_1_, f32[1024,128]{1,0:T(8,128)} %get-tuple-element.27.refs_1_, f32[1024,128]{1,0:T(8,128)} %get-tuple-element.28.refs_2_, f32[128,128]{1,0:T(8,128)} %get-tuple-element.29.refs_3_.refs_2_), custom_call_target="tpu_custom_call" | custom-call | flops 2147483648 | bytes 4194304 | tf_op jit(solution)/shard_map/scan/pallas_call | solution.py:71
  115.1 6.3 %all-to-all-start.3 = ((bf16[8,160,128]{2,1,0:T(8,128)(2,1)}), bf16[8,160,128]{2,1,0:T(8,128)(2,1)S(1)}, u32[]{:S(2)}, u32[]{:S(2)}) async-start(bf16[8,160,128]{2,1,0:T(8,128)(2,1)} %get-tuple-element.32), calls=%async_computation.3 | async-start | bytes 655360 | tf_op jit(solution)/shard_map/all_to_all | solution.py:415
  121.4 0.0 collective-permute-done.5.refs_1_
  121.4 3.3 %collective-permute-start.7 = (bf16[32,4096]{1,0:T(8,128)(2,1)S(1)}, bf16[32,4096]{1,0:T(8,128)(2,1)S(1)}, u32[]{:S(2)}, u32[]{:S(2)}) collective-permute-start(bf16[32,4096]{1,0:T(8,128)(2,1)S(1)} %slice.12), channel_id=1, source_target_pairs={{0,16},{16,32},{32,48},{48,0},{1,17},{17,33},{33,49},{49,1},{2,18}... | collective-permute-start | bytes 786440 | tf_op jit(solution)/shard_map/ppermute | solution.py:408
  124.7 0.0 collective-permute-done.6.refs_2_
  124.8 3.2 %collective-permute-start.8 = (bf16[32,4096]{1,0:T(8,128)(2,1)S(1)}, bf16[32,4096]{1,0:T(8,128)(2,1)S(1)}, u32[]{:S(2)}, u32[]{:S(2)}) collective-permute-start(bf16[32,4096]{1,0:T(8,128)(2,1)S(1)} %slice.13), channel_id=1, source_target_pairs={{0,48},{16,0},{32,16},{48,32},{1,49},{17,1},{33,17},{49,33},{2,50}... | collective-permute-start | bytes 786440 | tf_op jit(solution)/shard_map/ppermute | solution.py:409
  128.0 0.6 all-to-all-done.3.refs_1_
  128.6 1.3 group.1
  129.9 0.6 copy-done.2
  130.5 0.6 copy-done.3
  131.1 3.4 %all-to-all-start.4 = ((bf16[8,160,128]{2,1,0:T(8,128)(2,1)}), bf16[8,160,128]{2,1,0:T(8,128)(2,1)S(1)}, u32[]{:S(2)}, u32[]{:S(2)}) async-start(bf16[8,160,128]{2,1,0:T(8,128)(2,1)} %get-tuple-element.33), calls=%async_computation.4 | async-start | bytes 655360 | tf_op jit(solution)/shard_map/all_to_all | solution.py:423
  134.6 0.0 collective-permute-done.7.refs_3_
  134.6 0.0 copy-start.8
  134.6 0.0 collective-permute-done.8.refs_4_
  134.6 0.0 collective-permute-done.4.refs_1_.refs_5_
  134.6 0.6 copy-done.8
  135.3 0.1 copy-done.9
  135.4 7.7 %expand_rest.1 = (bf16[192,256]{1,0:T(8,128)(2,1)}, bf16[192,256]{1,0:T(8,128)(2,1)}) custom-call(bf16[64,4096]{1,0:T(8,128)(2,1)} %bitcast.12, bf16[64,4096]{1,0:T(8,128)(2,1)} %copy-done.5, bf16[64,4096]{1,0:T(8,128)(2,1)} %copy-done.6, bf16[32,4096]{1,0:T(8,128)(2,1)} %copy-done.8, bf16[32,4096]{1,0:T(8,128)(2,1)} %copy-done.9, ...), custom_call_target="tpu_custom_call" | custom-call | flops 1610612736 | bytes 4194304 | tf_op jit(solution)/shard_map/expand_rest/pallas_call | solution.py:71
  143.0 3.4 %collective-permute-start.10 = (bf16[192,256]{1,0:T(8,128)(2,1)}, bf16[192,256]{1,0:T(8,128)(2,1)S(1)}, u32[]{:S(2)}, u32[]{:S(2)}) collective-permute-start(bf16[192,256]{1,0:T(8,128)(2,1)} %get-tuple-element.43), channel_id=1, source_target_pairs={{0,8},{8,0},{1,9},{9,1},{2,10},{10,2},{3,11},{11,3},{4,12},{12,4},... | collective-permute-start | bytes 294920 | tf_op jit(solution)/shard_map/ppermute | solution.py:435
  146.5 0.0 all-gather.2.cloned.1.call-done.refs_0_
  146.5 8.1 %expand_first.1 = (bf16[192,384]{1,0:T(8,128)(2,1)}, bf16[192,384]{1,0:T(8,128)(2,1)}) custom-call(bf16[384,4096]{1,0:T(8,128)(2,1)} %all-gather.2.cloned.1.call-done.refs_0_, bf16[384,4096]{1,0:T(8,128)(2,1)} %collective-permute-done.4.refs_1_.refs_5_, bf16[384,4096]{1,0:T(8,128)(2,1)} %pad_maximum_fusion.refs_2_.refs_6_), custom_call_target="tpu_custom_call" | custom-call | flops 2415919104 | bytes 4194304 | tf_op jit(solution)/shard_map/expand_first/pallas_call | solution.py:71
  154.6 1.9 %collective-permute-start.9 = (bf16[192,384]{1,0:T(8,128)(2,1)}, bf16[192,384]{1,0:T(8,128)(2,1)S(1)}, u32[]{:S(2)}, u32[]{:S(2)}) collective-permute-start(bf16[192,384]{1,0:T(8,128)(2,1)} %get-tuple-element.42), channel_id=1, source_target_pairs={{0,8},{8,0},{1,9},{9,1},{2,10},{10,2},{3,11},{11,3},{4,12},{12,4},... | collective-permute-start | bytes 442376 | tf_op jit(solution)/shard_map/ppermute | solution.py:436
  156.5 0.0 all-to-all-done.4.refs_2_
  156.5 0.0 copy-start.7
  156.6 0.7 copy-done.7
  157.3 5.7 %finish.1 = bf16[128,1024]{1,0:T(8,128)(2,1)} custom-call(s32[1]{0:T(128)} %bitcast.refs_0_, f32[32,128]{1,0:T(8,128)} %reduce_sum.9.refs_0_.refs_1_, bf16[8,160,128]{2,1,0:T(8,128)(2,1)} %copy-done.7, f32[128,128]{1,0:T(8,128)} %get-tuple-element.29.refs_3_.refs_2_, f32[128,128]{1,0:T(8,128)} %copy-done.2, f32[8,128]{1,0:T(8,128)} %copy-done.3, ...), custom_call_target="tpu_custom_call" | custom-call | flops 2147483648 | bytes 4194304 | tf_op jit(solution)/shard_map/finish/pallas_call | solution.py:71
  162.9 0.0 collective-permute-done.10.refs_5_
  163.0 0.0 collective-permute-done.9.refs_4_
  163.0 0.6 copy-done.15
  163.6 0.1 copy-done.11
  163.6 3.1 %order.1 = bf16[192,1280]{1,0:T(8,128)(2,1)} custom-call(s32[1]{0:T(128)} %bitcast.7.refs_0_, s32[1]{0:T(128)} %bitcast.8.refs_1_, bf16[192,384]{1,0:T(8,128)(2,1)} %get-tuple-element.40.refs_2_, bf16[192,256]{1,0:T(8,128)(2,1)} %get-tuple-element.41.refs_3_, bf16[192,384]{1,0:T(8,128)(2,1)} %copy-done.11, bf16[192,256]{1,0:T(8,128)(2,1)} %copy-done.15), custom_call_target="tpu_custom_call" | custom-call | flops 268435456 | bytes 4194304 | tf_op jit(solution)/shard_map/order/pallas_call | solution.py:71
  (20 shorter events, 0.1 us)
Async XLA Ops:
  10.7 21.3 %all-to-all-start = ((bf16[8,20,512]{2,1,0:T(8,128)(2,1)}), bf16[8,20,512]{2,1,0:T(8,128)(2,1)S(1)}, u32[]{:S(2)}, u32[]{:S(2)}) async-start(bf16[8,20,512]{2,1,0:T(8,128)(2,1)} %place.1), calls=%async_computation | async-start | bytes 393216 | tf_op jit(solution)/shard_map/all_to_all | solution.py:362
  18.4 128.1 %all-gather.2.cloned.1.call-start = ((), (), s32[]{:S(2)}) async-start(), calls=%async_computation.5 | async-start | bytes 3538944 | tf_op jit(solution)/shard_map/all_gather | solution.py:401
  19.2 8.7 %collective-permute-start = (bf16[3,1024]{1,0:T(4,128)(2,1)S(1)}, bf16[3,1024]{1,0:T(4,128)(2,1)S(1)}, u32[]{:S(2)}, u32[]{:S(2)}) collective-permute-start(bf16[3,1024]{1,0:T(4,128)(2,1)S(1)} %slice.9), channel_id=1, source_target_pairs={{0,8},{8,16},{16,24},{24,32},{32,40},{40,48},{48,56},{56,64},{64,7... | collective-permute-start | bytes 18440 | tf_op jit(solution)/shard_map/ppermute | solution.py:356
  23.1 3.9 %copy-start.10 = (bf16[1024,32]{0,1:T(8,128)(2,1)S(1)}, bf16[1024,32]{0,1:T(8,128)(2,1)}, u32[]{:S(2)}) copy-start(bf16[1024,32]{0,1:T(8,128)(2,1)} %param.16) | copy-start | bytes 196612
  27.9 0.6 copy-start.16
  32.6 15.8 %copy-start = (bf16[12,4096]{1,0:T(8,128)(2,1)}, bf16[12,4096]{1,0:T(8,128)(2,1)S(1)}, u32[]{:S(2)}) copy-start(bf16[12,4096]{1,0:T(8,128)(2,1)S(1)} %get-tuple-element.39.refs_0_) | copy-start | bytes 294916
  32.6 10.2 %collective-permute-start.1 = (bf16[12,4096]{1,0:T(8,128)(2,1)S(1)}, bf16[12,4096]{1,0:T(8,128)(2,1)S(1)}, u32[]{:S(2)}, u32[]{:S(2)}) collective-permute-start(bf16[12,4096]{1,0:T(8,128)(2,1)S(1)} %get-tuple-element.39.refs_0_), channel_id=1, source_target_pairs={{0,16},{16,32},{32,48},{48,0},{1,17},{17,33},{33,49},{49,1},{2,18}... | collective-permute-start | bytes 294920 | tf_op jit(solution)/shard_map/ppermute | solution.py:391
  35.7 7.2 %collective-permute-start.2 = (bf16[12,4096]{1,0:T(8,128)(2,1)S(1)}, bf16[12,4096]{1,0:T(8,128)(2,1)S(1)}, u32[]{:S(2)}, u32[]{:S(2)}) collective-permute-start(bf16[12,4096]{1,0:T(8,128)(2,1)S(1)} %get-tuple-element.39.refs_0_), channel_id=1, source_target_pairs={{0,48},{16,0},{32,16},{48,32},{1,49},{17,1},{33,17},{49,33},{2,50}... | collective-permute-start | bytes 294920 | tf_op jit(solution)/shard_map/ppermute | solution.py:391
  39.7 8.6 %collective-permute-start.3 = (bf16[12,4096]{1,0:T(8,128)(2,1)S(1)}, bf16[12,4096]{1,0:T(8,128)(2,1)S(1)}, u32[]{:S(2)}, u32[]{:S(2)}) collective-permute-start(bf16[12,4096]{1,0:T(8,128)(2,1)S(1)} %get-tuple-element.39.refs_0_), channel_id=1, source_target_pairs={{0,32},{16,48},{32,0},{48,16},{1,33},{17,49},{33,1},{49,17},{2,34}... | collective-permute-start | bytes 294920 | tf_op jit(solution)/shard_map/ppermute | solution.py:391
  42.8 5.5 %copy-start.12 = (bf16[12,4096]{1,0:T(8,128)(2,1)}, bf16[12,4096]{1,0:T(8,128)(2,1)S(1)}, u32[]{:S(2)}) copy-start(bf16[12,4096]{1,0:T(8,128)(2,1)S(1)} %collective-permute-done.1.refs_1_) | copy-start | bytes 294916
  42.9 5.4 %copy-start.13 = (bf16[12,4096]{1,0:T(8,128)(2,1)}, bf16[12,4096]{1,0:T(8,128)(2,1)S(1)}, u32[]{:S(2)}) copy-start(bf16[12,4096]{1,0:T(8,128)(2,1)S(1)} %collective-permute-done.2.refs_2_) | copy-start | bytes 294916
  48.4 0.7 copy-start.14
  51.0 83.6 %collective-permute-start.4 = (bf16[384,4096]{1,0:T(8,128)(2,1)}, bf16[384,4096]{1,0:T(8,128)(2,1)}, u32[]{:S(2)}, u32[]{:S(2)}) collective-permute-start(bf16[384,4096]{1,0:T(8,128)(2,1)} %pad_maximum_fusion.refs_2_.refs_6_), channel_id=1, source_target_pairs={{0,8},{8,0},{1,9},{9,1},{2,10},{10,2},{3,11},{11,3},{4,12},{12,4},... | collective-permute-start | bytes 9437192 | tf_op jit(solution)/shard_map/ppermute | solution.py:364
  101.5 13.6 %copy-start.4 = (bf16[8,8,4096]{2,1,0:T(8,128)(2,1)}, bf16[8,8,4096]{2,1,0:T(8,128)(2,1)S(1)}, u32[]{:S(2)}) copy-start(bf16[8,8,4096]{2,1,0:T(8,128)(2,1)S(1)} %all_to_all.26) | copy-start | bytes 1572868
  101.5 19.9 %collective-permute-start.5 = (bf16[64,4096]{1,0:T(8,128)(2,1)S(1)}, bf16[64,4096]{1,0:T(8,128)(2,1)S(1)}, u32[]{:S(2)}, u32[]{:S(2)}) collective-permute-start(bf16[64,4096]{1,0:T(8,128)(2,1)S(1)} %bitcast.10), channel_id=1, source_target_pairs={{0,16},{16,32},{32,48},{48,0},{1,17},{17,33},{33,49},{49,1},{2,18}... | collective-permute-start | bytes 1572872 | tf_op jit(solution)/shard_map/ppermute | solution.py:407
  103.4 21.3 %collective-permute-start.6 = (bf16[64,4096]{1,0:T(8,128)(2,1)S(1)}, bf16[64,4096]{1,0:T(8,128)(2,1)S(1)}, u32[]{:S(2)}, u32[]{:S(2)}) collective-permute-start(bf16[64,4096]{1,0:T(8,128)(2,1)S(1)} %bitcast.11), channel_id=1, source_target_pairs={{0,48},{16,0},{32,16},{48,32},{1,49},{17,1},{33,17},{49,33},{2,50}... | collective-permute-start | bytes 1572872 | tf_op jit(solution)/shard_map/ppermute | solution.py:407
  108.0 20.6 %copy-start.1 = (f32[128,128]{1,0:T(8,128)S(1)}, f32[128,128]{1,0:T(8,128)}, u32[]{:S(2)}) copy-start(f32[128,128]{1,0:T(8,128)} %get-tuple-element.29.refs_3_.refs_2_) | copy-start | bytes 196612
  115.1 13.6 %all-to-all-start.3 = ((bf16[8,160,128]{2,1,0:T(8,128)(2,1)}), bf16[8,160,128]{2,1,0:T(8,128)(2,1)S(1)}, u32[]{:S(2)}, u32[]{:S(2)}) async-start(bf16[8,160,128]{2,1,0:T(8,128)(2,1)} %get-tuple-element.32), calls=%async_computation.3 | async-start | bytes 655360 | tf_op jit(solution)/shard_map/all_to_all | solution.py:415
  121.4 13.2 %copy-start.5 = (bf16[64,4096]{1,0:T(8,128)(2,1)}, bf16[64,4096]{1,0:T(8,128)(2,1)S(1)}, u32[]{:S(2)}) copy-start(bf16[64,4096]{1,0:T(8,128)(2,1)S(1)} %collective-permute-done.5.refs_1_) | copy-start | bytes 1572868
  121.4 13.1 %collective-permute-start.7 = (bf16[32,4096]{1,0:T(8,128)(2,1)S(1)}, bf16[32,4096]{1,0:T(8,128)(2,1)S(1)}, u32[]{:S(2)}, u32[]{:S(2)}) collective-permute-start(bf16[32,4096]{1,0:T(8,128)(2,1)S(1)} %slice.12), channel_id=1, source_target_pairs={{0,16},{16,32},{32,48},{48,0},{1,17},{17,33},{33,49},{49,1},{2,18}... | collective-permute-start | bytes 786440 | tf_op jit(solution)/shard_map/ppermute | solution.py:408
  124.7 9.9 %copy-start.6 = (bf16[64,4096]{1,0:T(8,128)(2,1)}, bf16[64,4096]{1,0:T(8,128)(2,1)S(1)}, u32[]{:S(2)}) copy-start(bf16[64,4096]{1,0:T(8,128)(2,1)S(1)} %collective-permute-done.6.refs_2_) | copy-start | bytes 1572868
  124.8 9.8 %collective-permute-start.8 = (bf16[32,4096]{1,0:T(8,128)(2,1)S(1)}, bf16[32,4096]{1,0:T(8,128)(2,1)S(1)}, u32[]{:S(2)}, u32[]{:S(2)}) collective-permute-start(bf16[32,4096]{1,0:T(8,128)(2,1)S(1)} %slice.13), channel_id=1, source_target_pairs={{0,48},{16,0},{32,16},{48,32},{1,49},{17,1},{33,17},{49,33},{2,50}... | collective-permute-start | bytes 786440 | tf_op jit(solution)/shard_map/ppermute | solution.py:409
  129.9 0.6 copy-start.2
  130.5 0.6 copy-start.3
  131.1 25.4 %all-to-all-start.4 = ((bf16[8,160,128]{2,1,0:T(8,128)(2,1)}), bf16[8,160,128]{2,1,0:T(8,128)(2,1)S(1)}, u32[]{:S(2)}, u32[]{:S(2)}) async-start(bf16[8,160,128]{2,1,0:T(8,128)(2,1)} %get-tuple-element.33), calls=%async_computation.4 | async-start | bytes 655360 | tf_op jit(solution)/shard_map/all_to_all | solution.py:423
  134.6 0.7 copy-start.8
  134.6 0.8 copy-start.9
  143.0 19.9 %collective-permute-start.10 = (bf16[192,256]{1,0:T(8,128)(2,1)}, bf16[192,256]{1,0:T(8,128)(2,1)S(1)}, u32[]{:S(2)}, u32[]{:S(2)}) collective-permute-start(bf16[192,256]{1,0:T(8,128)(2,1)} %get-tuple-element.43), channel_id=1, source_target_pairs={{0,8},{8,0},{1,9},{9,1},{2,10},{10,2},{3,11},{11,3},{4,12},{12,4},... | collective-permute-start | bytes 294920 | tf_op jit(solution)/shard_map/ppermute | solution.py:435
  154.6 8.4 %collective-permute-start.9 = (bf16[192,384]{1,0:T(8,128)(2,1)}, bf16[192,384]{1,0:T(8,128)(2,1)S(1)}, u32[]{:S(2)}, u32[]{:S(2)}) collective-permute-start(bf16[192,384]{1,0:T(8,128)(2,1)} %get-tuple-element.42), channel_id=1, source_target_pairs={{0,8},{8,0},{1,9},{9,1},{2,10},{10,2},{3,11},{11,3},{4,12},{12,4},... | collective-permute-start | bytes 442376 | tf_op jit(solution)/shard_map/ppermute | solution.py:436
  156.5 0.7 copy-start.7
  163.0 0.6 copy-start.15
  163.0 0.7 copy-start.11
Sparse Core Ops, SparseCore 0:
  51.2 62.2 all-gather.1

commit v4 on v1

--- a/solution.py
+++ b/solution.py
@@ -1,5 +1,3 @@
-import functools
-
 import jax
 import jax.numpy as jnp
 from jax import lax
@@ -16,25 +14,62 @@
 
 VMEM = pl.BlockSpec(memory_space=pltpu.VMEM)
 SMEM = pl.BlockSpec(memory_space=pltpu.SMEM)
-
-
-def call(kernel, out_shape, in_specs, scratch=(), name=None):
-    return pl.pallas_call(
-        kernel,
-        out_shape=out_shape,
-        in_specs=in_specs,
-        out_specs=jax.tree.map(lambda _: VMEM, out_shape),
-        scratch_shapes=scratch,
-        name=name,
-        compiler_params=pltpu.CompilerParams(vmem_limit_bytes=48 << 20),
-    )
+WHOLE = pl.BlockSpec(memory_space=pltpu.HBM)
+
+
+def call(kernel, out_shape, in_specs, scratch=(), name=None, vmem=60, flops=0):
+    single = not isinstance(out_shape, tuple)
+    outs = (out_shape,) if single else out_shape
+
+    def run(*operands):
+        moved = [index for index in range(len(in_specs)) if in_specs[index] is WHOLE]
+        buffers = [pltpu.VMEM(operands[index].shape, operands[index].dtype) for index in moved]
+        buffers += [pltpu.VMEM(out.shape, out.dtype) for out in outs]
+        count = len(operands)
+
+        def body(*refs):
+            inputs, results = list(refs[:count]), refs[count : count + len(outs)]
+            held = refs[count + len(outs) : count + len(outs) + len(buffers)]
+            rest, sems = refs[count + len(outs) + len(buffers) : -1], refs[-1]
+            copies = []
+            for place, index in enumerate(moved):
+                copies.append(pltpu.make_async_copy(inputs[index], held[place], sems.at[place]))
+                inputs[index] = held[place]
+            for copy in copies:
+                copy.start()
+            for copy in copies:
+                copy.wait()
+            made = held[len(moved) :]
+            kernel(*inputs, *made, *rest)
+            copies = [
+                pltpu.make_async_copy(source, target, sems.at[len(moved) + place])
+                for place, (source, target) in enumerate(zip(made, results))
+            ]
+            for copy in copies:
+                copy.start()
+            for copy in copies:
+                copy.wait()
+
+        found = pl.pallas_call(
+            body,
+            out_shape=outs,
+            in_specs=in_specs,
+            out_specs=(WHOLE,) * len(outs),
+            scratch_shapes=[*buffers, *scratch, pltpu.SemaphoreType.DMA((len(buffers),))],
+            name=name,
+            compiler_params=pltpu.CompilerParams(vmem_limit_bytes=vmem << 20),
+            cost_estimate=pl.CostEstimate(flops=flops, transcendentals=0, bytes_accessed=4 << 20),
+        )(*operands)
+        return found[0] if single else found
+
+    return run
 
 
 def shape(dims, dtype):
     return jax.ShapeDtypeStruct(dims, dtype)
 
 
-def place_kernel(routes_ref, tokens_ref, out_ref):
+def place_kernel(routes_ref, tokens_ref, out_ref, wide):
     rows = tokens_ref.shape[0]
     column = lax.broadcasted_iota(jnp.int32, (rows, 256), 1)
     expert, slot = column >> 5, column & 31
@@ -50,9 +85,88 @@
     table = jnp.where(named & (before == slot.astype(F32)), 1.0, 0.0).astype(BF16)
     placed = lax.dot_general(
         table, tokens_ref[...], (((0,), (0,)), ((), ())), preferred_element_type=F32
-    ).astype(BF16)
+    )
     for index in range(8):
-        out_ref[index] = placed[index * 32 : index * 32 + CAP]
+        rows = placed[index * 32 : index * 32 + CAP]
+        wide[:CAP, :], wide[CAP:, :] = rows[:, :256], rows[:, 256:]
+        packed = wide[...].astype(BF16)
+        for copy in range(4):
+            out_ref[index * 4 + copy] = packed
+
+
+def assemble_kernel(got_ref, out_ref, wide):
+    for index in range(32):
+        rows = got_ref[index].astype(F32)
+        here = pl.ds(index % 4 * CAP, CAP)
+        start = index // 4 * 512
+        wide[here, start : start + 256] = rows[:CAP]
+        wide[here, start + 256 : start + 512] = rows[CAP:]
+    out_ref[...] = wide[...].astype(BF16)
+
+
+def expand_kernel(rows_ref, weight_ref, out_ref, rows, weight, hidden, sems):
+    count = rows.shape[0]
+    chunks = [(start, min(256, count - start)) for start in range(0, count, 256)]
+    copies = [pltpu.make_async_copy(weight_ref, weight, sems.at[0])]
+    for index, (start, size) in enumerate(chunks):
+        part = pl.ds(start, size)
+        copies.append(pltpu.make_async_copy(rows_ref.at[part], rows.at[part], sems.at[1 + index]))
+    for copy in copies:
+        copy.start()
+    copies[0].wait()
+    units = hidden.shape[0]
+    for copy, (start, size) in zip(copies[1:], chunks):
+        copy.wait()
+        both = lax.dot_general(
+            weight[...],
+            rows[start : start + size, :],
+            (((1,), (1,)), ((), ())),
+            preferred_element_type=F32,
+        )
+        hidden[:, start : start + size] = (silu(both[:units]) * both[units:]).astype(BF16)
+    copy = pltpu.make_async_copy(hidden, out_ref, sems.at[0])
+    copy.start()
+    copy.wait()
+
+
+def expand(rows, weight, name):
+    units, count = weight.shape[0] // 2, rows.shape[0]
+    out = shape((units, count), BF16)
+    return pl.pallas_call(
+        expand_kernel,
+        out_shape=out,
+        in_specs=[WHOLE] * 2,
+        out_specs=WHOLE,
+        scratch_shapes=[
+            pltpu.VMEM(rows.shape, BF16),
+            pltpu.VMEM(weight.shape, BF16),
+            pltpu.VMEM(out.shape, BF16),
+            pltpu.SemaphoreType.DMA((1 + pl.cdiv(count, 256),)),
+        ],
+        name=name,
+        compiler_params=pltpu.CompilerParams(vmem_limit_bytes=60 << 20),
+        cost_estimate=pl.CostEstimate(
+            flops=4 * units * count * 4096, transcendentals=0, bytes_accessed=8 << 20
+        ),
+    )(rows, weight)
+
+
+def divided(value, by):
+    return (value * (65536 // by + 1)) >> 16
+
+
+def order_kernel(core_ref, mine_ref, other_ref, out_ref):
+    columns = out_ref.shape[1]
+    count = mine_ref.shape[1]
+    row = lax.broadcasted_iota(jnp.int32, (count, 1), 0)
+    block = divided(row, CAP)
+    base = row + (block + core_ref[0]) * CAP
+    column = lax.broadcasted_iota(jnp.int32, (count, columns), 1)
+    total = jnp.zeros(out_ref.shape, F32)
+    for ref, target in ((mine_ref, base), (other_ref, base + (1 - 2 * core_ref[0]) * CAP)):
+        table = jnp.where(column == target, 1.0, 0.0).astype(BF16)
+        total = total + jnp.dot(ref[...], table, preferred_element_type=F32)
+    out_ref[...] = total.astype(BF16)
 
 
 def silu(value):
@@ -214,13 +328,6 @@
         out_ref[:, lanes] = (value * silu(z_ref[:, lanes].astype(F32))).astype(BF16)
 
 
-def expand_rows(slot_rows, gate_matrix, up_matrix):
-    dims = (((1,), (1,)), ((), ()))
-    gate_part = lax.dot_general(gate_matrix, slot_rows, dims, preferred_element_type=F32)
-    up_part = lax.dot_general(up_matrix, slot_rows, dims, preferred_element_type=F32)
-    return (jax.nn.silu(gate_part) * up_part).astype(BF16)
-
-
 def shards(
     inner_x,
     inner_z,
@@ -238,11 +345,19 @@
     rows, width = inner_x.shape
     shards_of = lax.axis_size(SEQ)
     rim = lax.ppermute(inner_x[rows - 3 :], SEQ, [(i, i + 1) for i in range(shards_of - 1)])
-    placed = call(place_kernel, shape((8, CAP, moe_tokens.shape[1]), BF16), [VMEM] * 2, name="place")(
-        routes, moe_tokens
-    )
-    arrived = lax.all_to_all(placed, "exp", split_axis=0, concat_axis=2, tiled=True)
-    gathered = lax.all_gather(arrived[0], SEQ, axis=0, tiled=True)
+    swap = [(0, 1), (1, 0)]
+    features = moe_tokens.shape[1]
+    placed = call(
+        place_kernel,
+        shape((32, 2 * CAP, features // 2), BF16),
+        [WHOLE] * 2,
+        [pltpu.VMEM((2 * CAP, features // 2), F32)],
+        name="place",
+        flops=1 << 28,
+    )(routes, moe_tokens)
+    arrived = lax.all_to_all(placed, ("exp", "x"), split_axis=0, concat_axis=0, tiled=True)
+    weight = jnp.concatenate([gate_weight[0], up_weight[0]], axis=0)
+    other_weight = lax.ppermute(weight, "c", swap)
 
     dense = shape((rows * width // 128, 128), F32)
     conv, step, drive, rate, part = call(
@@ -254,34 +369,56 @@
             shape((128, 128), F32),
             shape((8, 32, rows), F32),
         ),
-        [VMEM] * 7,
+        [WHOLE] * 7,
         [pltpu.VMEM((rows + 8, width), F32)],
-        name="conv",
+        name="conv", flops=1 << 29,
     )(inner_x, rim, step_raw, conv_weight, state_proj, step_bias[None], decay_log)
+    arrived, _, _ = lax.optimization_barrier((arrived, part, weight))
+    block = call(
+        assemble_kernel,
+        shape((4 * CAP, 4096), BF16),
+        [WHOLE],
+        [pltpu.VMEM((4 * CAP, 4096), F32)],
+        name="assemble",
+        vmem=16,
+        flops=1 << 28,
+    )(arrived)
+    gathered = lax.all_gather(block, "z", axis=0, tiled=True)
     coef = jnp.sum(lax.all_to_all(part, "exp", split_axis=0, concat_axis=0, tiled=True), axis=0)
     packed = shape((8, 160, 128), BF16)
     local, sums, ends = call(
-        scan_kernel, (dense, dense, packed), [SMEM] + [VMEM] * 3, name="scan"
+        scan_kernel, (dense, dense, packed), [SMEM] + [WHOLE] * 3, name="scan", flops=1 << 31
     )(coef, step, drive, rate)
     near = lax.all_to_all(ends, ("x", "c"), split_axis=0, concat_axis=0, tiled=True)
     place_in = lax.axis_index(("x", "c")).astype(jnp.int32).reshape(1)
     before, before_step, whole = call(
         group_kernel,
         (shape((128, 128), F32), shape((8, 128), F32), packed),
-        [SMEM, VMEM, VMEM],
-        name="group",
+        [SMEM, WHOLE, WHOLE],
+        name="group", vmem=16, flops=1 << 28,
     )(place_in, near, rate)
     far = lax.all_to_all(whole, "z", split_axis=0, concat_axis=0, tiled=True)
+    far, other_weight = lax.optimization_barrier((far, other_weight))
     layer = lax.axis_index("z").astype(jnp.int32).reshape(1)
     mixed = call(
         finish_kernel,
         shape((rows, width), BF16),
-        [SMEM, SMEM] + [VMEM] * 9,
+        [SMEM, SMEM] + [WHOLE] * 9,
         [pltpu.VMEM(dense.shape, F32)],
-        name="finish",
+        name="finish", flops=1 << 31,
     )(layer, coef, far, rate, before, before_step, local, sums, conv, skip_gain[None], inner_z)
 
-    hidden = expand_rows(gathered, gate_weight[0], up_weight[0])[None]
+    gathered, mixed = lax.optimization_barrier((gathered, mixed))
+    other = lax.ppermute(expand(gathered, other_weight, "expand_other"), "c", swap)
+    mine = expand(gathered, weight, "expand_mine")
+    core = lax.axis_index("c").astype(jnp.int32).reshape(1)
+    hidden = call(
+        order_kernel,
+        shape((gate_weight.shape[1], 1280), BF16),
+        [SMEM, WHOLE, WHOLE],
+        name="order",
+        flops=1 << 28,
+    )(core, mine, other)[None]
     return mixed, hidden
 
 

time: 160 us -> 148 us (0.925)
  Pallas kernels: 11.6 us -> 39.6 us
  local copies, waits for them, and re-layouts: 27.8 us -> 6.32 us
  blocking collectives: 26.8 us -> 11.8 us
  starting transfers between devices: 24.2 us -> 37.3 us
  matrix products: 12.1 us -> 0 us
  waiting for transfers between devices: 42.3 us -> 33.7 us
  other arithmetic: 0.01 us -> 3.98 us
    pallas_call x5 -> x9, Pallas kernels: 11.6 us -> 39.6 us  [the longest x7 23.9 us: run(): pl.pallas_call(body, out_shape=outs, in_specs=in_specs, out_specs=(WHOLE,...]
    unnamed x34 -> x20, local copies, waits for them, and re-layouts: 27.1 us -> 5.6 us
    all_to_all x1 -> x0, blocking collectives: 16.2 us -> none  [shards(): lax.all_to_all(placed, 'exp', split_axis=0, concat_axis=2, tiled=True)]
    all_gather x1, waiting for transfers between devices: 18.8 us -> 4.78 us  [shards(): gathered = lax.all_gather(block, 'z', axis=0, tiled=True)]
    dot_general x2 -> x0, matrix products: 12.1 us -> none  [the longest x1 7.72 us: expand_rows(): lax.dot_general(gate_matrix, slot_rows, dims, preferred_element_type=F32)]
    all_to_all x0 -> x1, starting transfers between devices: none -> 10.5 us  [shards(): lax.all_to_all(placed, ('exp', 'x'), split_axis=0, concat_axis=0, tiled=T...]
    ppermute x0 -> x2, starting transfers between devices: none -> 6.95 us  [the longest x1 4.37 us: shards(): other_weight = lax.ppermute(weight, 'c', swap)]
    all_to_all x0 -> x1, waiting for transfers between devices: none -> 5.24 us  [shards(): lax.all_to_all(placed, ('exp', 'x'), split_axis=0, concat_axis=0, tiled=T...]
  transfers between devices with their start and end apart: 4 -> 7, of which waited for: 3 -> 4; matrix products, arithmetic and copies ran while one was open for 1% -> 4% of each run, Pallas kernels for 7% -> 17%
where the time goes in v4:
time: 148 us; the launch traced here: 147 us
  Pallas kernels  39.6 us (27%)
  starting transfers between devices  37.3 us (25%)
  waiting for transfers between devices  33.7 us (23%)
  between operations  14.2 us (10%)
  blocking collectives  11.8 us (8%)
  local copies, waits for them, and re-layouts  6.32 us (4%)
  other arithmetic  3.98 us (3%)
    pallas_call x7, Pallas kernels, run(): pl.pallas_call(body, out_shape=outs, in_specs=in_specs, out_specs=(WHOLE,...  23.9 us
    all_to_all x1, waiting for transfers between devices, shards(): far = lax.all_to_all(whole, 'z', split_axis=0, concat_axis=0, tiled=True)  16.5 us
    pallas_call x2, Pallas kernels, expand(): pl.pallas_call(expand_kernel, out_shape=out, in_specs=[WHOLE] * 2, out_sp...  15.7 us
    all_to_all x1, blocking collectives, shards(): lax.all_to_all(part, 'exp', split_axis=0, concat_axis=0, tiled=True)  11.8 us
    all_to_all x1, starting transfers between devices, shards(): lax.all_to_all(placed, ('exp', 'x'), split_axis=0, concat_axis=0, tiled=T...  10.5 us
    all_to_all x1, starting transfers between devices, shards(): far = lax.all_to_all(whole, 'z', split_axis=0, concat_axis=0, tiled=True)  10.1 us
    all_to_all x1, waiting for transfers between devices, shards(): lax.all_to_all(ends, ('x', 'c'), split_axis=0, concat_axis=0, tiled=True)  7.16 us
    unnamed x20, local copies, waits for them, and re-layouts  5.6 us
  transfers between devices with their start and end apart: 7, of which 4 were waited for; matrix products, arithmetic and copies ran while one was open for 4% of the time, Pallas kernels for 17%

profile of v4, /device:TPU:1, one launch (start us, length us, event | category | flops | bytes accessed | tf_op | source)
XLA Modules:
  0.0 147.0 jit_solution(17065307274022081938)
XLA Ops:
  7.2 0.0 copy-start.4
  7.2 1.5 %copy.14.refs_0_ = s32[128,2]{1,0:T(8,128)} copy(s32[128,2]{0,1:T(2,128)} %param.21) | data formatting | bytes 2048 | tf_op args[9]
  8.7 2.3 %place.1 = bf16[32,40,256]{2,1,0:T(8,128)(2,1)} custom-call(s32[128,2]{1,0:T(8,128)} %copy.14.refs_0_, bf16[128,512]{1,0:T(8,128)(2,1)} %refs_1_.1), custom_call_target="tpu_custom_call" | custom-call | flops 268435456 | bytes 4194304 | tf_op jit(solution)/shard_map/place/pallas_call | solution.py:53
  11.1 10.5 %all-to-all-start = ((bf16[32,40,256]{2,1,0:T(8,128)(2,1)}), bf16[32,40,256]{2,1,0:T(8,128)(2,1)S(1)}, u32[]{:S(2)}, u32[]{:S(2)}) async-start(bf16[32,40,256]{2,1,0:T(8,128)(2,1)} %place.1), calls=%async_computation | async-start | bytes 1310720 | tf_op jit(solution)/shard_map/all_to_all | solution.py:358
  21.6 0.0 all-gather.2.cloned.1.call-start
  21.6 0.7 slice.3
  22.4 4.2 %collective-permute-start = (bf16[3,1024]{1,0:T(4,128)(2,1)S(1)}, bf16[3,1024]{1,0:T(4,128)(2,1)S(1)}, u32[]{:S(2)}, u32[]{:S(2)}) collective-permute-start(bf16[3,1024]{1,0:T(4,128)(2,1)S(1)} %slice.3), channel_id=1, source_target_pairs={{0,8},{8,16},{16,24},{24,32},{32,40},{40,48},{48,56},{56,64},{64,7... | collective-permute-start | bytes 18440 | tf_op jit(solution)/shard_map/ppermute | solution.py:347
  26.6 0.0 copy-done.4
  26.6 0.0 copy-start.6
  26.6 3.4 %pad_maximum_fusion.weight_ref = bf16[384,4096]{1,0:T(8,128)(2,1)} fusion(bf16[192,4096]{1,0:T(8,128)(2,1)S(1)} %bitcast.8, bf16[192,4096]{1,0:T(8,128)(2,1)} %bitcast.9), kind=kLoop, calls=%fused_computation | loop fusion | flops 6291456 | bytes 6291456 | tf_op jit(solution)/shard_map/concatenate | solution.py:359
  30.0 0.0 copy-done.6
  30.0 0.8 copy.15.refs_4_
  30.8 0.0 collective-permute-done.refs_1_
  30.8 0.0 copy-start.8
  30.9 0.6 copy-done.8
  31.4 3.6 %conv.1 = (f32[128,1024]{1,0:T(8,128)}, f32[1024,128]{1,0:T(8,128)}, f32[1024,128]{1,0:T(8,128)}, f32[128,128]{1,0:T(8,128)}, f32[8,32,128]{2,1,0:T(8,128)}) custom-call(bf16[128,1024]{1,0:T(8,128)(2,1)} %refs_0_.2, bf16[3,1024]{1,0:T(4,128)(2,1)} %copy-done.8, bf16[128,1024]{1,0:T(8,128)(2,1)} %refs_2_.1, f32[4,1024]{1,0:T(4,128)} %refs_3_.1, ...), custom_call_target="tpu_custom_call" | custom-call | flops 536870912 | bytes 4194304 | tf_op jit(solution)/shard_map/conv/pallas_call | solution.py:53
  35.0 5.2 %all-to-all-done.refs_0_ = bf16[32,40,256]{2,1,0:T(8,128)(2,1)S(1)} async-done(((bf16[32,40,256]{2,1,0:T(8,128)(2,1)}), bf16[32,40,256]{2,1,0:T(8,128)(2,1)S(1)}, u32[]{:S(2)}, u32[]{:S(2)}) %all-to-all-start) | async-done | bytes 655392 | tf_op jit(solution)/shard_map/all_to_all | solution.py:358
  40.3 1.2 assemble.1
  41.5 0.0 all-gather.2.cloned.1.call-update
  41.5 4.4 %collective-permute-start.1 = (bf16[384,4096]{1,0:T(8,128)(2,1)}, bf16[384,4096]{1,0:T(8,128)(2,1)S(1)}, u32[]{:S(2)}, u32[]{:S(2)}) collective-permute-start(bf16[384,4096]{1,0:T(8,128)(2,1)} %pad_maximum_fusion.weight_ref), channel_id=1, source_target_pairs={{0,8},{8,0},{1,9},{9,1},{2,10},{10,2},{3,11},{11,3},{4,12},{12,4},... | collective-permute-start | bytes 9437192 | tf_op jit(solution)/shard_map/ppermute | solution.py:360
  45.9 11.8 %all_to_all.20 = f32[8,32,128]{2,1,0:T(8,128)S(1)} all-to-all(f32[8,32,128]{2,1,0:T(8,128)} %get-tuple-element.18), channel_id=1, replica_groups=mesh['z'=8,'x'=4,'c'=2,'exp'=8] {'exp'}, dimensions={0} | all-to-all | bytes 262144 | tf_op jit(solution)/shard_map/all_to_all | solution.py:387
  57.7 0.6 reduce_sum.9.refs_0_.refs_1_
  58.3 0.0 copy-start
  58.3 7.0 %scan.1 = (f32[1024,128]{1,0:T(8,128)}, f32[1024,128]{1,0:T(8,128)}, bf16[8,160,128]{2,1,0:T(8,128)(2,1)}) custom-call(f32[32,128]{1,0:T(8,128)} %reduce_sum.9.refs_0_.refs_1_, f32[1024,128]{1,0:T(8,128)} %get-tuple-element.20.refs_1_, f32[1024,128]{1,0:T(8,128)} %get-tuple-element.21.refs_2_, f32[128,128]{1,0:T(8,128)} %get-tuple-element.22.refs_3_.refs_2_), custom_call_target="tpu_custom_call" | custom-call | flops 2147483648 | bytes 4194304 | tf_op jit(solution)/shard_map/scan/pallas_call | solution.py:53
  65.4 5.5 %all-to-all-start.2 = ((bf16[8,160,128]{2,1,0:T(8,128)(2,1)}), bf16[8,160,128]{2,1,0:T(8,128)(2,1)S(1)}, u32[]{:S(2)}, u32[]{:S(2)}) async-start(bf16[8,160,128]{2,1,0:T(8,128)(2,1)} %get-tuple-element.23), calls=%async_computation.2 | async-start | bytes 655360 | tf_op jit(solution)/shard_map/all_to_all | solution.py:392
  70.8 7.2 %all-to-all-done.2.refs_1_ = bf16[8,160,128]{2,1,0:T(8,128)(2,1)S(1)} async-done(((bf16[8,160,128]{2,1,0:T(8,128)(2,1)}), bf16[8,160,128]{2,1,0:T(8,128)(2,1)S(1)}, u32[]{:S(2)}, u32[]{:S(2)}) %all-to-all-start.2) | async-done | bytes 327712 | tf_op jit(solution)/shard_map/all_to_all | solution.py:392
  78.0 0.0 copy-done
  78.0 1.3 group.1
  79.3 0.0 copy-start.1
  79.3 0.6 copy-done.1
  79.9 0.0 copy-start.2
  79.9 0.6 copy-done.2
  80.5 10.1 %all-to-all-start.3 = ((bf16[8,160,128]{2,1,0:T(8,128)(2,1)}), bf16[8,160,128]{2,1,0:T(8,128)(2,1)S(1)}, u32[]{:S(2)}, u32[]{:S(2)}) async-start(bf16[8,160,128]{2,1,0:T(8,128)(2,1)} %get-tuple-element.24), calls=%async_computation.3 | async-start | bytes 655360 | tf_op jit(solution)/shard_map/all_to_all | solution.py:400
  90.5 16.5 %all-to-all-done.3.refs_2_ = bf16[8,160,128]{2,1,0:T(8,128)(2,1)S(1)} async-done(((bf16[8,160,128]{2,1,0:T(8,128)(2,1)}), bf16[8,160,128]{2,1,0:T(8,128)(2,1)S(1)}, u32[]{:S(2)}, u32[]{:S(2)}) %all-to-all-start.3) | async-done | bytes 327712 | tf_op jit(solution)/shard_map/all_to_all | solution.py:400
  107.1 0.0 copy-start.5
  107.1 0.0 collective-permute-done.1.weight_ref
  107.1 0.0 copy-start.3
  107.1 0.7 copy-done.5
  107.8 5.7 %finish.1 = bf16[128,1024]{1,0:T(8,128)(2,1)} custom-call(s32[1]{0:T(128)} %bitcast.3.refs_0_, f32[32,128]{1,0:T(8,128)} %reduce_sum.9.refs_0_.refs_1_, bf16[8,160,128]{2,1,0:T(8,128)(2,1)} %copy-done.5, f32[128,128]{1,0:T(8,128)} %get-tuple-element.22.refs_3_.refs_2_, f32[128,128]{1,0:T(8,128)} %copy-done.1, f32[8,128]{1,0:T(8,128)} %copy-done.2, ...), custom_call_target="tpu_custom_call" | custom-call | flops 2147483648 | bytes 4194304 | tf_op jit(solution)/shard_map/finish/pallas_call | solution.py:53
  113.5 0.0 copy-done.3
  113.5 4.8 %all-gather.2.cloned.1.call-done.rows_ref = bf16[640,4096]{1,0:T(8,128)(2,1)} async-done(((bf16[80,4096]{1,0:T(8,128)(2,1)}), bf16[640,4096]{1,0:T(8,128)(2,1)}) %all-gather.2.cloned.1.call-update) | async-done | bytes 5242896 | tf_op jit(solution)/shard_map/all_gather | solution.py:386
  118.3 7.8 %expand_other.1 = bf16[192,640]{1,0:T(8,128)(2,1)} custom-call(bf16[640,4096]{1,0:T(8,128)(2,1)} %all-gather.2.cloned.1.call-done.rows_ref, bf16[384,4096]{1,0:T(8,128)(2,1)} %copy-done.3), custom_call_target="tpu_custom_call" | custom-call | flops 2013265920 | bytes 8388608 | tf_op jit(solution)/shard_map/expand_other/pallas_call | solution.py:135
  126.1 2.6 %collective-permute-start.2 = (bf16[192,640]{1,0:T(8,128)(2,1)}, bf16[192,640]{1,0:T(8,128)(2,1)S(1)}, u32[]{:S(2)}, u32[]{:S(2)}) collective-permute-start(bf16[192,640]{1,0:T(8,128)(2,1)} %expand_other.1), channel_id=1, source_target_pairs={{0,8},{8,0},{1,9},{9,1},{2,10},{10,2},{3,11},{11,3},{4,12},{12,4},... | collective-permute-start | bytes 737288 | tf_op jit(solution)/shard_map/ppermute | solution.py:412
  128.7 7.9 %expand_mine.1.refs_1_ = bf16[192,640]{1,0:T(8,128)(2,1)} custom-call(bf16[640,4096]{1,0:T(8,128)(2,1)} %all-gather.2.cloned.1.call-done.rows_ref, bf16[384,4096]{1,0:T(8,128)(2,1)} %pad_maximum_fusion.weight_ref), custom_call_target="tpu_custom_call" | custom-call | flops 2013265920 | bytes 8388608 | tf_op jit(solution)/shard_map/expand_mine/pallas_call | solution.py:135
  136.6 0.0 collective-permute-done.2.refs_2_
  136.6 0.0 copy-start.7
  136.6 0.7 copy-done.7
  137.3 2.8 %order.1 = bf16[192,1280]{1,0:T(8,128)(2,1)} custom-call(s32[1]{0:T(128)} %bitcast.6.refs_0_, bf16[192,640]{1,0:T(8,128)(2,1)} %expand_mine.1.refs_1_, bf16[192,640]{1,0:T(8,128)(2,1)} %copy-done.7), custom_call_target="tpu_custom_call" | custom-call | flops 268435456 | bytes 4194304 | tf_op jit(solution)/shard_map/order/pallas_call | solution.py:53
Async XLA Ops:
  7.2 19.4 %copy-start.4 = (bf16[1,192,4096]{2,1,0:T(8,128)(2,1)S(1)}, bf16[1,192,4096]{2,1,0:T(8,128)(2,1)}, u32[]{:S(2)}) copy-start(bf16[1,192,4096]{2,1,0:T(8,128)(2,1)} %param.23) | copy-start | bytes 4718596
  11.1 29.2 %all-to-all-start = ((bf16[32,40,256]{2,1,0:T(8,128)(2,1)}), bf16[32,40,256]{2,1,0:T(8,128)(2,1)S(1)}, u32[]{:S(2)}, u32[]{:S(2)}) async-start(bf16[32,40,256]{2,1,0:T(8,128)(2,1)} %place.1), calls=%async_computation | async-start | bytes 1310720 | tf_op jit(solution)/shard_map/all_to_all | solution.py:358
  21.6 96.7 %all-gather.2.cloned.1.call-start = ((), (), s32[]{:S(2)}) async-start(), calls=%async_computation.4 | async-start | bytes 5898240 | tf_op jit(solution)/shard_map/all_gather | solution.py:386
  22.4 8.5 %collective-permute-start = (bf16[3,1024]{1,0:T(4,128)(2,1)S(1)}, bf16[3,1024]{1,0:T(4,128)(2,1)S(1)}, u32[]{:S(2)}, u32[]{:S(2)}) collective-permute-start(bf16[3,1024]{1,0:T(4,128)(2,1)S(1)} %slice.3), channel_id=1, source_target_pairs={{0,8},{8,16},{16,24},{24,32},{32,40},{40,48},{48,56},{56,64},{64,7... | collective-permute-start | bytes 18440 | tf_op jit(solution)/shard_map/ppermute | solution.py:347
  26.6 3.4 %copy-start.6 = (bf16[1024,32]{0,1:T(8,128)(2,1)S(1)}, bf16[1024,32]{0,1:T(8,128)(2,1)}, u32[]{:S(2)}) copy-start(bf16[1024,32]{0,1:T(8,128)(2,1)} %param.16) | copy-start | bytes 196612
  30.8 0.6 copy-start.8
  41.5 65.6 %collective-permute-start.1 = (bf16[384,4096]{1,0:T(8,128)(2,1)}, bf16[384,4096]{1,0:T(8,128)(2,1)S(1)}, u32[]{:S(2)}, u32[]{:S(2)}) collective-permute-start(bf16[384,4096]{1,0:T(8,128)(2,1)} %pad_maximum_fusion.weight_ref), channel_id=1, source_target_pairs={{0,8},{8,0},{1,9},{9,1},{2,10},{10,2},{3,11},{11,3},{4,12},{12,4},... | collective-permute-start | bytes 9437192 | tf_op jit(solution)/shard_map/ppermute | solution.py:360
  58.3 19.7 %copy-start = (f32[128,128]{1,0:T(8,128)S(1)}, f32[128,128]{1,0:T(8,128)}, u32[]{:S(2)}) copy-start(f32[128,128]{1,0:T(8,128)} %get-tuple-element.22.refs_3_.refs_2_) | copy-start | bytes 196612
  65.4 12.7 %all-to-all-start.2 = ((bf16[8,160,128]{2,1,0:T(8,128)(2,1)}), bf16[8,160,128]{2,1,0:T(8,128)(2,1)S(1)}, u32[]{:S(2)}, u32[]{:S(2)}) async-start(bf16[8,160,128]{2,1,0:T(8,128)(2,1)} %get-tuple-element.23), calls=%async_computation.2 | async-start | bytes 655360 | tf_op jit(solution)/shard_map/all_to_all | solution.py:392
  79.3 0.6 copy-start.1
  79.9 0.6 copy-start.2
  80.5 26.6 %all-to-all-start.3 = ((bf16[8,160,128]{2,1,0:T(8,128)(2,1)}), bf16[8,160,128]{2,1,0:T(8,128)(2,1)S(1)}, u32[]{:S(2)}, u32[]{:S(2)}) async-start(bf16[8,160,128]{2,1,0:T(8,128)(2,1)} %get-tuple-element.24), calls=%async_computation.3 | async-start | bytes 655360 | tf_op jit(solution)/shard_map/all_to_all | solution.py:400
  107.1 0.7 copy-start.5
  107.1 6.4 %copy-start.3 = (bf16[384,4096]{1,0:T(8,128)(2,1)}, bf16[384,4096]{1,0:T(8,128)(2,1)S(1)}, u32[]{:S(2)}) copy-start(bf16[384,4096]{1,0:T(8,128)(2,1)S(1)} %collective-permute-done.1.weight_ref) | copy-start | bytes 9437188
  126.1 10.5 %collective-permute-start.2 = (bf16[192,640]{1,0:T(8,128)(2,1)}, bf16[192,640]{1,0:T(8,128)(2,1)S(1)}, u32[]{:S(2)}, u32[]{:S(2)}) collective-permute-start(bf16[192,640]{1,0:T(8,128)(2,1)} %expand_other.1), channel_id=1, source_target_pairs={{0,8},{8,0},{1,9},{9,1},{2,10},{10,2},{3,11},{11,3},{4,12},{12,4},... | collective-permute-start | bytes 737288 | tf_op jit(solution)/shard_map/ppermute | solution.py:412
  136.6 0.7 copy-start.7
Sparse Core Ops, SparseCore 0:
  41.6 76.5 all-gather.1
